TPU v7x, 128 devices: a whole 4x4x4 slice. The times are simulated.
128 devices in a mesh: dp: 4 (over y_hi, core), ctx: 32 (over x, y_lo, z).
Axes of the slice: x: 4, y: 4 (y_hi: 2, y_lo: 2; y = y_hi * 2 + y_lo), z: 4, core: 2. Of those that a mesh axis runs over, the one named last changes fastest.
Arguments:
- queries: bfloat16 [16384, 2048], P(('dp', 'ctx')), parts along dimension 0, may hold values from -9 to 9
- keys: bfloat16 [16384, 512], P(('dp', 'ctx')), parts along dimension 0, may hold values from -9 to 9
- values: bfloat16 [16384, 512], P(('dp', 'ctx')), parts along dimension 0, may hold values from -6 to 6
- grad_out: bfloat16 [16384, 2048], P(('dp', 'ctx')), parts along dimension 0, may hold values from -6 to 6
- positions: int32 [1024], P('dp'), parts along dimension 0, may hold values from 0 to 4095, as said below
Outputs:
- attended: bfloat16 [16384, 2048], P(('dp', 'ctx')), parts along dimension 0
- grad_queries: bfloat16 [16384, 2048], P(('dp', 'ctx')), parts along dimension 0
- grad_keys: bfloat16 [16384, 512], P(('dp', 'ctx')), parts along dimension 0
- grad_values: bfloat16 [16384, 512], P(('dp', 'ctx')), parts along dimension 0
There are 4 independent parts, one for each index of `dp`. A program takes and returns all parts, laid end to end along the dimension named above; each array names one. Nothing has to cross between parts.
Inputs may be any that keep to these rules, and one draw needn't show every extreme that they name: 256 distinct token positions in increasing order; the 128 tokens of one index of ctx hold at most 32 of them, and one index holds exactly 32.
All inputs are finite; a program needn't handle non-finite values.
Results may differ from a plain program's by a relative error of at most 0.0075.
Values may be sent and summed in bfloat16 or wider, within the bound.
No kernel may reach another device: no remote copies, remote signals or barrier semaphores. Data moves between devices by JAX's collectives and lax.ppermute only.
A program may use at most 192 MiB of HBM per device.

v0:
```python
import functools
import math

import jax
import jax.numpy as jnp
from jax import lax
from jax.experimental import pallas as pl
from jax.experimental.pallas import tpu as pltpu
from jax.sharding import PartitionSpec as P


HQ = 16
HK = 4
DH = 128
BLOCK = 64
CAP = 32
REP = HQ // HK
GROUP = 4
SIDES = 2
XS = 4
CHUNK = 64
ROWS = REP * BLOCK
WIDE = REP * DH
KV = 2 * DH
PIECES = 2 * WIDE // KV
SCALE = 1.0 / math.sqrt(DH)
EXP2 = SCALE * math.log2(math.e)
NEG = -1e30

F32 = jnp.float32
BF16 = jnp.bfloat16


def dot_nt(a, b):
    return lax.dot_general(a, b, (((1,), (1,)), ((), ())), preferred_element_type=F32)


def dot_nn(a, b):
    return lax.dot_general(a, b, (((1,), (0,)), ((), ())), preferred_element_type=F32)


def iota(shape, dim):
    return lax.broadcasted_iota(jnp.int32, shape, dim)


def hot(mask):
    return mask.astype(F32).astype(BF16)


def split(x):
    high = x.astype(BF16)
    return high, (x - high.astype(F32)).astype(BF16)


def place():
    me = lax.axis_index("ctx")
    cluster = me // GROUP
    return me, cluster // SIDES, lax.rem(cluster, SIDES), lax.rem(me, GROUP)


def column(row):
    n = row.shape[1]
    eye = iota((n, n), 0) == iota((n, n), 1)
    wide = jnp.where(eye, jnp.broadcast_to(row, (n, n)), 0).astype(F32)
    return jnp.sum(wide, axis=1, keepdims=True).astype(jnp.int32)


def below(pos_row, edge):
    return jnp.sum((pos_row < edge).astype(F32), axis=1, keepdims=True).astype(jnp.int32)


def pair_count(pos_row, x, toks):
    size = SIDES * GROUP * toks
    inside = (pos_row >= x * size) & (pos_row < (x + 1) * size)
    return jnp.sum(inside.astype(F32)).astype(jnp.int32)


def slots_along_lanes(pos_col, tok_row, before):
    is_row = jnp.sum((pos_col == tok_row).astype(F32), axis=0, keepdims=True)
    rank = jnp.sum((pos_col < tok_row).astype(F32), axis=0, keepdims=True).astype(jnp.int32)
    return jnp.where(is_row > 0.5, rank - before, -1)


def slots_along_rows(pos_row, tok_col, before):
    is_col = jnp.sum((pos_row == tok_col).astype(F32), axis=1, keepdims=True)
    rank = jnp.sum((pos_row < tok_col).astype(F32), axis=1, keepdims=True).astype(jnp.int32)
    return jnp.where(is_col > 0.5, rank - before, -1)


def prep_kernel(toks, pos_any, q_any, k_any, v_any, g_any, *refs):
    zs_refs, qg_refs, pos_out = refs[:GROUP], refs[GROUP : 2 * GROUP], refs[2 * GROUP]
    picked, pos_ref, q_ref, g_ref, k_ref, v_ref, sems = refs[2 * GROUP + 1 :]
    pos_copy = pltpu.make_async_copy(pos_any, pos_ref, sems.at[4])
    pos_copy.start()
    copies = [
        pltpu.make_async_copy(src, dst, sems.at[i])
        for i, (src, dst) in enumerate(((q_any, q_ref), (g_any, g_ref), (k_any, k_ref), (v_any, v_ref)))
    ]
    for copy in copies:
        copy.start()
    me, _, _, z = place()
    pos_copy.wait()
    pos_row = pos_ref[...]
    pos_out[...] = pos_row
    first = me * toks
    slot = slots_along_lanes(column(pos_row), first + iota((1, toks), 1), below(pos_row, first))
    pick = hot(slot == iota((CAP, toks), 0))
    width = HQ * DH
    for copy in copies:
        copy.wait()
    picked[:, :width] = dot_nn(pick, q_ref[...]).astype(BF16)
    picked[:, width:] = dot_nn(pick, g_ref[...]).astype(BF16)
    for step in range(GROUP):
        j = lax.rem(z + step, GROUP)
        head = pl.ds(pl.multiple_of(j * DH, DH), DH)
        cols = pl.ds(pl.multiple_of(j * WIDE, WIDE), WIDE)
        zs_refs[step][:toks, :DH] = k_ref[:, head]
        zs_refs[step][:toks, DH:] = v_ref[:, head]
        for p in range(PIECES):
            base = j * WIDE + p * KV if p * KV < WIDE else width + j * WIDE + p * KV - WIDE
            part = picked[:, pl.ds(pl.multiple_of(base, KV), KV)]
            zs_refs[step][toks + CAP * p : toks + CAP * (p + 1), :] = part
        qg_refs[step][:, :WIDE] = q_ref[:, cols]
        qg_refs[step][:, WIDE:] = g_ref[:, cols]


def join_kernel(toks, *refs):
    zs_refs, kv_ref, qc_ref = refs[:GROUP], refs[GROUP], refs[GROUP + 1]
    _, _, _, z = place()
    for step in range(GROUP):
        src = lax.rem(z + GROUP - step, GROUP)
        kv_ref[pl.ds(pl.multiple_of(src * toks, toks), toks), :] = zs_refs[step][:toks, :]
        rows = PIECES * CAP
        qc_ref[pl.ds(pl.multiple_of(src * rows, rows), rows), :] = zs_refs[step][toks:, :]


def side_first(x, y, m, ctoks):
    return (lax.rem(x + XS - m, XS) * SIDES + y) * ctoks


def pick_kernel(ctoks, pos_ref, *refs):
    kv_refs, out_ref = refs[:XS], refs[XS]
    _, x, y, _ = place()
    pos_row = pos_ref[...]
    glob = pos_row.shape[1]
    pos_col = column(pos_row)
    got = jnp.zeros((glob, KV), F32)
    for m in range(XS):
        first = side_first(x, y, m, ctoks)
        got = got + dot_nn(hot(pos_col == first + iota((glob, ctoks), 1)), kv_refs[m][...])
    out_ref[:glob, :] = got.astype(BF16)
    end = slice(ctoks - BLOCK, ctoks)
    out_ref[glob : glob + BLOCK, :] = jnp.where(y == 0, kv_refs[0][end, :], kv_refs[1][end, :])
    out_ref[glob + BLOCK : glob + 2 * BLOCK, :] = jnp.where(
        y == 0, kv_refs[3][:BLOCK, :], kv_refs[0][:BLOCK, :]
    )


def fill_slots(y, slots, mine_ref, peer_ref):
    half = GROUP * CAP
    rows = PIECES * CAP
    for ref, side in ((mine_ref, y), (peer_ref, 1 - y)):
        for d in range(GROUP):
            at = pl.ds(pl.multiple_of(side * half + d * CAP, CAP), CAP)
            for p in range(PIECES):
                begin = d * rows + p * CAP
                slots[at, p * KV : (p + 1) * KV] = ref[begin : begin + CAP, :]


def padded_ranks(x, toks, pos_col, before):
    lane = iota((1, 2 * GROUP * CAP), 1)
    dev = x * (SIDES * GROUP) + lane // CAP
    start = jnp.sum((pos_col < dev * toks).astype(F32), axis=0, keepdims=True).astype(jnp.int32)
    stop = jnp.sum((pos_col < (dev + 1) * toks).astype(F32), axis=0, keepdims=True).astype(jnp.int32)
    rank = start + lax.rem(lane, CAP)
    return jnp.where(rank < stop, rank - before, -1)


def chunk_rows(slots, ranks, base):
    pick = hot(ranks == base + iota((CHUNK, ranks.shape[1]), 0))
    got = dot_nn(pick, slots[...]).astype(BF16)
    q = jnp.concatenate([got[:, h * DH : (h + 1) * DH] for h in range(REP)], axis=0)
    g = jnp.concatenate([got[:, WIDE + h * DH : WIDE + (h + 1) * DH] for h in range(REP)], axis=0)
    return q, g


def stats_kernel(toks, pos_ref, *refs):
    kv_refs, mine_ref, peer_ref, out_ref = refs[:XS], refs[XS], refs[XS + 1], refs[XS + 2]
    slots, sc = refs[XS + 3 :]
    _, x, y, _ = place()
    pos_row = pos_ref[...]
    before = below(pos_row, x * (SIDES * GROUP * toks))
    fill_slots(y, slots, mine_ref, peer_ref)
    ranks = padded_ranks(x, toks, column(pos_row), before)
    ctoks = GROUP * toks
    out_ref[...] = jnp.zeros_like(out_ref)

    def chunk(ch, carry):
        q, g = chunk_rows(slots, ranks, ch * CHUNK)
        top = jnp.full((1, ROWS), NEG, F32)
        for m in range(XS):
            s = dot_nt(kv_refs[m][:, :DH], q)
            sc[m * ctoks : (m + 1) * ctoks, :] = s
            top = jnp.maximum(top, jnp.max(s, axis=0, keepdims=True))
        total = jnp.zeros((1, ROWS), F32)
        dsum = jnp.zeros((1, ROWS), F32)
        for m in range(XS):
            w = jnp.exp2((sc[m * ctoks : (m + 1) * ctoks, :] - top) * EXP2)
            total = total + jnp.sum(w, axis=0, keepdims=True)
            dsum = dsum + jnp.sum(w * dot_nt(kv_refs[m][:, DH:], g), axis=0, keepdims=True)
        out_ref[ch, 0:1, :] = top
        out_ref[ch, 1:2, :] = total
        out_ref[ch, 2:3, :] = dsum
        return carry

    lax.fori_loop(0, (pair_count(pos_row, x, toks) + CHUNK - 1) // CHUNK, chunk, 0)


def near_kernel(seq, toks, pos_ref, after_ref, kv_ref, e2_ref, e2p_ref, *refs):
    qg_in = refs[:GROUP]
    outs = refs[GROUP : 2 * GROUP]
    dw_ref, dkg_ref, e5_ref, win, dwin, kg, kgt, qg, out = refs[2 * GROUP :]
    me, _, _, z = place()
    ctoks = GROUP * toks
    pos_row = pos_ref[...]
    glob = pos_row.shape[1]
    pos_col = column(pos_row)
    first = (me // GROUP) * ctoks
    win[:BLOCK, :] = e2p_ref[glob : glob + BLOCK, :]
    win[BLOCK : BLOCK + ctoks, :] = kv_ref[...]
    win[BLOCK + ctoks :, :] = e2p_ref[glob + BLOCK :, :]
    both = (e2_ref[:glob, :].astype(F32) + e2p_ref[:glob, :].astype(F32)).astype(BF16)
    kg[...] = both
    kgt[...] = both.T
    for step in range(GROUP):
        src = lax.rem(z + GROUP - step, GROUP)
        qg[pl.ds(pl.multiple_of(src * toks, toks), toks), :] = qg_in[step][...]
    dwin[...] = jnp.zeros_like(dwin)
    dkg_ref[...] = jnp.zeros_like(dkg_ref)

    def block(b, carry):
        base = first + b * BLOCK
        here = pl.ds(pl.multiple_of(b * BLOCK, BLOCK), 3 * BLOCK)
        mine = pl.ds(pl.multiple_of(b * BLOCK, BLOCK), BLOCK)
        kn, vn = win[here, :DH], win[here, DH:]
        q = jnp.concatenate([qg[mine, h * DH : (h + 1) * DH] for h in range(REP)], axis=0)
        g = jnp.concatenate([qg[mine, WIDE + h * DH : WIDE + (h + 1) * DH] for h in range(REP)], axis=0)
        key_tok = base - BLOCK + iota((3 * BLOCK, 1), 0)
        key_glob = jnp.sum((key_tok == pos_row).astype(F32), axis=1, keepdims=True)
        usable = (key_tok >= 0) & (key_tok < seq) & (key_glob < 0.5)
        row_tok = base + lax.rem(iota((1, ROWS), 1), BLOCK)
        live = 1.0 - jnp.sum((pos_col == row_tok).astype(F32), axis=0, keepdims=True)

        sn = jnp.where(usable, dot_nt(kn, q), NEG)
        sf = dot_nt(kg[:, :DH], q)
        top = jnp.maximum(jnp.max(sn, axis=0, keepdims=True), jnp.max(sf, axis=0, keepdims=True))
        wn = jnp.exp2((sn - top) * EXP2)
        wf = jnp.exp2((sf - top) * EXP2)
        dn = dot_nt(vn, g)
        df = dot_nt(kg[:, DH:], g)
        total = jnp.sum(wn, axis=0, keepdims=True) + jnp.sum(wf, axis=0, keepdims=True)
        dsum = jnp.sum(wn * dn, axis=0, keepdims=True) + jnp.sum(wf * df, axis=0, keepdims=True)
        inv = 1.0 / total
        delta = dsum * inv
        mixed = (dot_nn(vn.T, wn.astype(BF16)) + dot_nn(kgt[DH:, :], wf.astype(BF16))) * inv
        inv_live = inv * live
        pn = wn * inv_live
        pf = wf * inv_live
        dsn = (pn * (dn - delta)).astype(BF16)
        dsf = (pf * (df - delta)).astype(BF16)
        gq = (dot_nn(kn.T, dsn) + dot_nn(kgt[:DH, :], dsf)) * SCALE
        dwin[here, :DH] += dot_nn(dsn, q) * SCALE
        dwin[here, DH:] += dot_nn(pn.astype(BF16), g)
        dkg_ref[:, :DH] += dot_nn(dsf, q) * SCALE
        dkg_ref[:, DH:] += dot_nn(pf.astype(BF16), g)
        att = mixed.T.astype(BF16)
        gqr = gq.T.astype(BF16)
        for h in range(REP):
            rows = slice(h * BLOCK, (h + 1) * BLOCK)
            out[mine, h * DH : (h + 1) * DH] = att[rows]
            out[mine, WIDE + h * DH : WIDE + (h + 1) * DH] = gqr[rows]
        return carry

    lax.fori_loop(0, ctoks // BLOCK, block, 0)
    for step in range(GROUP):
        dst = lax.rem(z + step, GROUP)
        outs[step][...] = out[pl.ds(pl.multiple_of(dst * toks, toks), toks), :]
    dw_ref[...] = dwin[BLOCK : BLOCK + ctoks, :]
    e5_ref[:glob, :] = dkg_ref[...].astype(BF16)
    e5_ref[glob : glob + BLOCK, :] = dwin[:BLOCK, :].astype(BF16)
    e5_ref[glob + BLOCK :, :] = dwin[BLOCK + ctoks :, :].astype(BF16)


def grads_kernel(toks, pos_ref, *refs):
    kv_refs, refs = refs[:XS], refs[XS:]
    mine_ref, peer_ref, st_ref, stp_ref, dw_ref, dkg_ref = refs[:6]
    dkv, e4_ref, keep_ref, slots, kvt, rows_out = refs[6:]
    _, x, y, _ = place()
    ctoks = GROUP * toks
    pos_row = pos_ref[...]
    glob = pos_row.shape[1]
    pos_col = column(pos_row)
    pair_first = x * (SIDES * ctoks)
    before = below(pos_row, pair_first)
    count = pair_count(pos_row, x, toks)
    fill_slots(y, slots, mine_ref, peer_ref)
    ranks = padded_ranks(x, toks, pos_col, before)
    rows_out[...] = jnp.zeros_like(rows_out)
    for m in range(XS):
        kvt[m] = kv_refs[m][...].T

    far_high, far_low = split(dkg_ref[...])
    for m in range(XS):
        first = side_first(x, y, m, ctoks)
        mask = hot(first + iota((ctoks, glob), 0) == pos_row)
        whole = dot_nn(mask, far_high) + dot_nn(mask, far_low)
        dkv[m] = whole + dw_ref[...] if m == 0 else whole

    def chunk(ch, carry):
        base = ch * CHUNK
        q, g = chunk_rows(slots, ranks, base)
        valid = (base + lax.rem(iota((1, ROWS), 1), CHUNK) < count).astype(F32)
        here, there = st_ref[ch], stp_ref[ch]
        top = jnp.maximum(here[0:1], there[0:1])
        a = jnp.exp2((here[0:1] - top) * EXP2)
        b = jnp.exp2((there[0:1] - top) * EXP2)
        inv = 1.0 / (here[1:2] * a + there[1:2] * b)
        delta = (here[2:3] * a + there[2:3] * b) * inv
        inv = inv * valid
        att = jnp.zeros((DH, ROWS), F32)
        gq = jnp.zeros((DH, ROWS), F32)
        for m in range(XS):
            p = jnp.exp2((dot_nt(kv_refs[m][:, :DH], q) - top) * EXP2) * inv
            p_high, p_low = split(p)
            ds = (p * (dot_nt(kv_refs[m][:, DH:], g) - delta)).astype(BF16)
            dkv[m, :, :DH] += dot_nn(ds, q) * SCALE
            dkv[m, :, DH:] += dot_nn(p_high, g)
            vt = kvt[m, DH:, :]
            att = att + dot_nn(vt, p_high) + dot_nn(vt, p_low)
            gq = gq + dot_nn(kvt[m, :DH, :], ds)
        att = att.T
        gq = (gq * SCALE).T
        rows = pl.ds(pl.multiple_of(base, CHUNK), CHUNK)
        for h in range(REP):
            part = slice(h * CHUNK, (h + 1) * CHUNK)
            rows_out[rows, h * DH : (h + 1) * DH] = att[part]
            rows_out[rows, WIDE + h * DH : WIDE + (h + 1) * DH] = gq[part]
        return carry

    lax.fori_loop(0, (count + CHUNK - 1) // CHUNK, chunk, 0)
    part_high, part_low = split(rows_out[...])
    slot = iota((GROUP * CAP, 2 * GROUP * CAP), 0)
    lane = iota((GROUP * CAP, 2 * GROUP * CAP), 1)

    def cluster_mask(side):
        begin = below(pos_row, pair_first + side * ctoks) - before
        size = below(pos_row, pair_first + (side + 1) * ctoks) - before - begin
        return hot((lane == begin + slot) & (slot < size))

    e4_ref[...] = dot_nn(cluster_mask(1 - y), part_high).astype(BF16)
    mask = cluster_mask(y)
    keep_ref[...] = dot_nn(mask, part_high) + dot_nn(mask, part_low)


def peer_kernel(toks, pos_ref, dkv_ref, e5p_ref, own_ref, *send_refs):
    _, x, y, _ = place()
    ctoks = GROUP * toks
    pos_row = pos_ref[...]
    glob = pos_row.shape[1]
    far = e5p_ref[:glob, :]
    low = e5p_ref[glob : glob + BLOCK, :].astype(F32)
    high = e5p_ref[glob + BLOCK :, :].astype(F32)
    at_zero = (y == 0).astype(F32)
    at_one = 1.0 - at_zero
    none = jnp.zeros((ctoks - BLOCK, KV), F32)
    edges = {
        0: jnp.concatenate([high * at_one, none[BLOCK:], low * at_zero], axis=0),
        1: jnp.concatenate([none, low * at_one], axis=0),
        3: jnp.concatenate([high * at_zero, none], axis=0),
    }
    for m in range(XS):
        first = side_first(x, y, m, ctoks)
        mask = hot(first + iota((ctoks, glob), 0) == pos_row)
        whole = dkv_ref[m] + dot_nn(mask, far)
        if m in edges:
            whole = whole + edges[m]
        if m == 0:
            own_ref[...] = whole
        else:
            send_refs[XS - m - 1][...] = whole.astype(BF16)


def merge_kernel(toks, pos_ref, own_ref, *refs):
    got_refs, refs = refs[: XS - 1], refs[XS - 1 :]
    keep_ref, e4p_ref = refs[0], refs[1]
    zs_refs, whole = refs[2 : 2 + GROUP], refs[2 + GROUP]
    me, _, _, z = place()
    pos_row = pos_ref[...]
    total = own_ref[...]
    for ref in got_refs:
        total = total + ref[...].astype(F32)
    whole[...] = total.astype(BF16)
    rows = (keep_ref[...] + e4p_ref[...].astype(F32)).astype(BF16)
    first_dev = (me // GROUP) * GROUP
    before = below(pos_row, first_dev * toks)
    slot = iota((CAP, GROUP * CAP), 0)
    lane = iota((CAP, GROUP * CAP), 1)
    for step in range(GROUP):
        j = lax.rem(z + step, GROUP)
        zs_refs[step][:toks, :] = whole[pl.ds(pl.multiple_of(j * toks, toks), toks), :]
        begin = below(pos_row, (first_dev + j) * toks) - before
        size = below(pos_row, (first_dev + j + 1) * toks) - before - begin
        got = dot_nn(hot((lane == begin + slot) & (slot < size)), rows).astype(BF16)
        for p in range(PIECES):
            zs_refs[step][toks + CAP * p : toks + CAP * (p + 1), :] = got[:, p * KV : (p + 1) * KV]


def post_kernel(toks, pos_ref, *refs):
    zs_refs, o_refs = refs[:GROUP], refs[GROUP : 2 * GROUP]
    att_ref, gq_ref, dk_ref, dv_ref = refs[2 * GROUP :]
    me, _, _, z = place()
    pos_row = pos_ref[...]
    first = me * toks
    slot = slots_along_rows(pos_row, first + iota((toks, 1), 0), below(pos_row, first))
    mask = hot(slot == iota((toks, CAP), 1))
    is_glob = slot >= 0
    for step in range(GROUP):
        j = lax.rem(z + GROUP - step, GROUP)
        head = pl.ds(pl.multiple_of(j * DH, DH), DH)
        dk_ref[:, head] = zs_refs[step][:toks, :DH]
        dv_ref[:, head] = zs_refs[step][:toks, DH:]
        for p in range(PIECES):
            rows = zs_refs[step][toks + CAP * p : toks + CAP * (p + 1), :]
            placed = dot_nn(mask, rows)
            here = o_refs[step][:, p * KV : (p + 1) * KV].astype(F32)
            value = jnp.where(is_glob, placed, here).astype(BF16)
            ref, off = (att_ref, p * KV) if p * KV < WIDE else (gq_ref, p * KV - WIDE)
            ref[:, pl.ds(pl.multiple_of(j * WIDE + off, KV), KV)] = value


VM = pl.BlockSpec(memory_space=pltpu.VMEM)
HBM = pl.BlockSpec(memory_space=pltpu.HBM)


def call(kernel, outs, args, scratch=(), specs=None, sems=0, flops=0, moved=0):
    return pl.pallas_call(
        kernel,
        out_shape=tuple(jax.ShapeDtypeStruct(s, d) for s, d in outs),
        in_specs=specs or [VM] * len(args),
        out_specs=(VM,) * len(outs),
        scratch_shapes=[pltpu.VMEM(s, d) for s, d in scratch] + [pltpu.SemaphoreType.DMA((sems,))] * (sems > 0),
        compiler_params=pltpu.CompilerParams(vmem_limit_bytes=40 * 1024 * 1024),
        cost_estimate=pl.CostEstimate(flops=flops, bytes_accessed=moved, transcendentals=0),
    )(*args)


def local(queries, keys, values, grad_out, positions):
    toks, width = queries.shape
    kwidth = keys.shape[1]
    devices = lax.axis_size("ctx")
    seq = toks * devices
    ctoks = GROUP * toks
    glob = positions.shape[0]
    zrows = toks + PIECES * CAP
    part = ((toks, 2 * WIDE), BF16)
    zpart = ((zrows, KV), BF16)
    cpart = ((ctoks, KV), BF16)
    ppart = ((glob + 2 * BLOCK, KV), BF16)

    def zperm(a, step):
        pairs = [(c, c // GROUP * GROUP + (c + step) % GROUP) for c in range(devices)]
        return lax.ppermute(a, "ctx", pairs)

    def xperm(a, step):
        return lax.ppermute(a, "ctx", [(c, (c + step * SIDES * GROUP) % devices) for c in range(devices)])

    def yperm(a):
        return lax.ppermute(a, "ctx", [(c, c ^ GROUP) for c in range(devices)])

    sent = call(
        functools.partial(prep_kernel, toks),
        [zpart] * GROUP + [part] * GROUP + [((1, glob), jnp.int32)],
        tuple(pltpu.with_memory_space_constraint(a, pltpu.HBM) for a in (positions.reshape(1, glob), queries, keys, values, grad_out)),
        scratch=[
            ((CAP, 2 * width), BF16),
            ((1, glob), jnp.int32),
            ((toks, width), BF16),
            ((toks, width), BF16),
            ((toks, kwidth), BF16),
            ((toks, kwidth), BF16),
        ],
        specs=[HBM] * 5,
        sems=5,
        moved=4 << 20,
    )
    pos = sent[2 * GROUP]
    zs = [sent[0]] + [zperm(sent[step], step) for step in range(1, GROUP)]
    kv0, qc = call(
        functools.partial(join_kernel, toks), [cpart, ((GROUP * PIECES * CAP, KV), BF16)], tuple(zs), moved=1 << 20
    )
    kvs = [kv0] + [xperm(kv0, m) for m in range(1, XS)]
    qcp = yperm(qc)
    qgs = [sent[GROUP]] + [zperm(sent[GROUP + step], step) for step in range(1, GROUP)]
    (e2,) = call(functools.partial(pick_kernel, ctoks), [ppart], (pos, *kvs), moved=6 << 20)
    e2p = yperm(e2)
    (st,) = call(
        functools.partial(stats_kernel, toks),
        [((glob // CHUNK, 8, ROWS), F32)],
        (pos, *kvs, qc, qcp),
        scratch=[((2 * GROUP * CAP, 2 * WIDE), BF16), ((XS * ctoks, ROWS), F32)],
        moved=14 << 20,
    )
    stp = yperm(st)
    *outs, dw, dkg, e5 = call(
        functools.partial(near_kernel, seq, toks),
        [part] * GROUP + [((ctoks, KV), F32), ((glob, KV), F32), ppart],
        (pos, st, kv0, e2, e2p, *qgs),
        scratch=[
            ((ctoks + 2 * BLOCK, KV), BF16),
            ((ctoks + 2 * BLOCK, KV), F32),
            ((glob, KV), BF16),
            ((KV, glob), BF16),
            ((ctoks, 2 * WIDE), BF16),
            ((ctoks, 2 * WIDE), BF16),
        ],
        moved=40 << 20,
    )
    e5p = yperm(e5)
    os = [outs[0]] + [zperm(outs[step], step) for step in range(1, GROUP)]
    dkv, e4, keep = call(
        functools.partial(grads_kernel, toks),
        [((XS, ctoks, KV), F32), ((GROUP * CAP, 2 * WIDE), BF16), ((GROUP * CAP, 2 * WIDE), F32)],
        (pos, *kvs, qc, qcp, st, stp, dw, dkg),
        scratch=[
            ((2 * GROUP * CAP, 2 * WIDE), BF16),
            ((XS, KV, ctoks), BF16),
            ((2 * GROUP * CAP, 2 * WIDE), F32),
        ],
        moved=24 << 20,
    )
    own, *sends = call(
        functools.partial(peer_kernel, toks),
        [((ctoks, KV), F32)] + [cpart] * (XS - 1),
        (pos, dkv, e5p),
        moved=3 << 20,
    )
    got = [xperm(sends[m - 1], m) for m in range(1, XS)]
    e4p = yperm(e4)
    zback = call(
        functools.partial(merge_kernel, toks),
        [zpart] * GROUP,
        (pos, own, *got, keep, e4p),
        scratch=[((ctoks, KV), BF16)],
        moved=3 << 20,
    )
    zr = [zback[0]] + [zperm(zback[step], step) for step in range(1, GROUP)]
    return call(
        functools.partial(post_kernel, toks),
        [((toks, width), BF16)] * 2 + [((toks, kwidth), BF16)] * 2,
        (pos, *zr, *os),
        moved=4 << 20,
    )


def solution(mesh):
    rows = P(("dp", "ctx"), None)
    return jax.shard_map(
        local,
        mesh=mesh,
        in_specs=(rows, rows, rows, rows, P("dp")),
        out_specs=(rows, rows, rows, rows),
        check_vma=False,
    )
```

profile of v0, /device:TPU:0, one launch (start us, length us, event | category | flops | bytes accessed | tf_op | source)
XLA Modules:
  0.0 83.1 jit_solution(10855266171440125936)
XLA Ops:
  0.6 1.6 %shard_map.84 = (bf16[256,256]{1,0:T(8,128)(2,1)S(1)}, bf16[256,256]{1,0:T(8,128)(2,1)S(1)}, bf16[256,256]{1,0:T(8,128)(2,1)S(1)}, bf16[256,256]{1,0:T(8,128)(2,...) custom-call(s32[1,256]{1,0:T(1,128)} %bitcast.1, ...), custom_call_target="tpu_custom_call" | custom-call | bytes 4194304 | tf_op jit(solution)/shard_map/pallas_call | solution.py:446
  2.3 2.1 %collective-permute-start = (bf16[256,256]{1,0:T(8,128)(2,1)S(1)}, bf16[256,256]{1,0:T(8,128)(2,1)S(1)}, u32[]{:S(2)}, u32[]{:S(2)}) collective-permute-start(bf16[256,256]{1,0:T(8,128)(2,1)S(1)} %get-tuple-element.35), channel_id=1, source_target_pairs={{0,1},{1,2},{2,3},{3,0},{4,5},{5,6},{6,7},{7,4},{8,9},{9,10},{10,1... | collective-permute-start | bytes 393224 | tf_op jit(solution)/shard_map/ppermute | solution.py:472
  4.4 3.6 %collective-permute-start.1 = (bf16[256,256]{1,0:T(8,128)(2,1)S(1)}, bf16[256,256]{1,0:T(8,128)(2,1)S(1)}, u32[]{:S(2)}, u32[]{:S(2)}) collective-permute-start(bf16[256,256]{1,0:T(8,128)(2,1)S(1)} %get-tuple-element.36), channel_id=1, source_target_pairs={{0,2},{1,3},{2,0},{3,1},{4,6},{5,7},{6,4},{7,5},{8,10},{9,11},{10,... | collective-permute-start | bytes 393224 | tf_op jit(solution)/shard_map/ppermute | solution.py:472
  10.0 4.0 %collective-permute-done.1.refs_2_ = bf16[256,256]{1,0:T(8,128)(2,1)S(1)} collective-permute-done((bf16[256,256]{1,0:T(8,128)(2,1)S(1)}, bf16[256,256]{1,0:T(8,128)(2,1)S(1)}, u32[]{:S(2)}, u32[]{:S(2)}) %collective-permute-start.1) | collective-permute-done | bytes 131104 | tf_op jit(solution)/shard_map/ppermute | solution.py:472
  14.0 2.8 %collective-permute-start.5 = (bf16[512,256]{1,0:T(8,128)(2,1)S(1)}, bf16[512,256]{1,0:T(8,128)(2,1)S(1)}, u32[]{:S(2)}, u32[]{:S(2)}) collective-permute-start(bf16[512,256]{1,0:T(8,128)(2,1)S(1)} %get-tuple-element.38.refs_0_.kv_ref), channel_id=1, source_target_pairs={{0,24},{1,25},{2,26},{3,27},{4,28},{5,29},{6,30},{7,31},{8,0},{9,1... | collective-permute-start | bytes 786440 | tf_op jit(solution)/shard_map/ppermute | solution.py:475
  21.4 5.9 %collective-permute-done.5.refs_3_ = bf16[512,256]{1,0:T(8,128)(2,1)S(1)} collective-permute-done((bf16[512,256]{1,0:T(8,128)(2,1)S(1)}, bf16[512,256]{1,0:T(8,128)(2,1)S(1)}, u32[]{:S(2)}, u32[]{:S(2)}) %collective-permute-start.5) | collective-permute-done | bytes 262176 | tf_op jit(solution)/shard_map/ppermute | solution.py:475
  27.2 2.0 %collective-permute-start.10 = (bf16[128,1024]{1,0:T(8,128)(2,1)S(1)}, bf16[128,1024]{1,0:T(8,128)(2,1)S(1)}, u32[]{:S(2)}, u32[]{:S(2)}) collective-permute-start(bf16[128,1024]{1,0:T(8,128)(2,1)S(1)} %get-tuple-element.42), channel_id=1, source_target_pairs={{0,2},{1,3},{2,0},{3,1},{4,6},{5,7},{6,4},{7,5},{8,10},{9,11},{10,... | collective-permute-start | bytes 786440 | tf_op jit(solution)/shard_map/ppermute | solution.py:472
  29.2 2.6 %collective-permute-start.11 = (bf16[128,1024]{1,0:T(8,128)(2,1)S(1)}, bf16[128,1024]{1,0:T(8,128)(2,1)S(1)}, u32[]{:S(2)}, u32[]{:S(2)}) collective-permute-start(bf16[128,1024]{1,0:T(8,128)(2,1)S(1)} %get-tuple-element.43), channel_id=1, source_target_pairs={{0,3},{1,0},{2,1},{3,2},{4,7},{5,4},{6,5},{7,6},{8,11},{9,8},{10,9... | collective-permute-start | bytes 786440 | tf_op jit(solution)/shard_map/ppermute | solution.py:472
  32.3 1.7 %collective-permute-start.8 = (bf16[384,256]{1,0:T(8,128)(2,1)S(1)}, bf16[384,256]{1,0:T(8,128)(2,1)S(1)}, u32[]{:S(2)}, u32[]{:S(2)}) collective-permute-start(bf16[384,256]{1,0:T(8,128)(2,1)S(1)} %shard_map.87.e2_ref), channel_id=1, source_target_pairs={{0,4},{1,5},{2,6},{3,7},{4,0},{5,1},{6,2},{7,3},{8,12},{9,13},{10,... | collective-permute-start | bytes 589832 | tf_op jit(solution)/shard_map/ppermute | solution.py:478
  35.2 2.7 %collective-permute-done.11.refs_3_ = bf16[128,1024]{1,0:T(8,128)(2,1)S(1)} collective-permute-done((bf16[128,1024]{1,0:T(8,128)(2,1)S(1)}, bf16[128,1024]{1,0:T(8,128)(2,1)S(1)}, u32[]{:S(2)}, u32[]{:S(2)}) %collective-permute-start.11) | collective-permute-done | bytes 262176 | tf_op jit(solution)/shard_map/ppermute | solution.py:472
  38.3 6.5 %shard_map.88 = (bf16[128,1024]{1,0:T(8,128)(2,1)S(1)}, bf16[128,1024]{1,0:T(8,128)(2,1)S(1)}, bf16[128,1024]{1,0:T(8,128)(2,1)S(1)}, bf16[128,1024]{1,0:T(8,128...) custom-call(s32[1,256]{1,0:T(1,128)S(1)} %get-tuple-element.33.pos_ref, ...), custom_call_target="tpu_custom_call" | custom-call | bytes 41943040 | tf_op jit(solution)/shard_map/pallas_call | solution.py:446
  44.8 1.7 %collective-permute-start.12 = (bf16[384,256]{1,0:T(8,128)(2,1)S(1)}, bf16[384,256]{1,0:T(8,128)(2,1)S(1)}, u32[]{:S(2)}, u32[]{:S(2)}) collective-permute-start(bf16[384,256]{1,0:T(8,128)(2,1)S(1)} %get-tuple-element.47), channel_id=1, source_target_pairs={{0,4},{1,5},{2,6},{3,7},{4,0},{5,1},{6,2},{7,3},{8,12},{9,13},{10,... | collective-permute-start | bytes 589832 | tf_op jit(solution)/shard_map/ppermute | solution.py:478
  46.9 4.0 %collective-permute-done.7.refs_7_ = f32[4,8,256]{2,1,0:T(8,128)S(1)} collective-permute-done((f32[4,8,256]{2,1,0:T(8,128)S(1)}, f32[4,8,256]{2,1,0:T(8,128)S(1)}, u32[]{:S(2)}, u32[]{:S(2)}) %collective-permute-start.7) | collective-permute-done | bytes 32800 | tf_op jit(solution)/shard_map/ppermute | solution.py:478
  50.9 3.5 %shard_map.89 = (f32[4,512,256]{2,1,0:T(8,128)S(1)}, bf16[128,1024]{1,0:T(8,128)(2,1)S(1)}, f32[128,1024]{1,0:T(8,128)S(1)}) custom-call(s32[1,256]{1,0:T(1,128)S(1)} %get-tuple-element.33.pos_ref, bf16[512,256]{1,0:T(8,128)(2,1)S(1)} %get-tuple-element.38.refs_0_.kv_ref, bf16[512,256]{1,0:T(8,128)(2,1)S(1)} %collective-permute-done.3.refs_1_, ...), custom_call_target="tpu_custom_call" | custom-call | bytes 25165824 | tf_op jit(solution)/shard_map/pallas_call | solution.py:446
  54.4 1.6 %collective-permute-start.16 = (bf16[128,1024]{1,0:T(8,128)(2,1)S(1)}, bf16[128,1024]{1,0:T(8,128)(2,1)S(1)}, u32[]{:S(2)}, u32[]{:S(2)}) collective-permute-start(bf16[128,1024]{1,0:T(8,128)(2,1)S(1)} %get-tuple-element.53), channel_id=1, source_target_pairs={{0,4},{1,5},{2,6},{3,7},{4,0},{5,1},{6,2},{7,3},{8,12},{9,13},{10,... | collective-permute-start | bytes 786440 | tf_op jit(solution)/shard_map/ppermute | solution.py:478
  56.5 2.3 %collective-permute-start.13 = (bf16[512,256]{1,0:T(8,128)(2,1)S(1)}, bf16[512,256]{1,0:T(8,128)(2,1)S(1)}, u32[]{:S(2)}, u32[]{:S(2)}) collective-permute-start(bf16[512,256]{1,0:T(8,128)(2,1)S(1)} %get-tuple-element.49), channel_id=1, source_target_pairs={{0,8},{1,9},{2,10},{3,11},{4,12},{5,13},{6,14},{7,15},{8,16},{9,17... | collective-permute-start | bytes 786440 | tf_op jit(solution)/shard_map/ppermute | solution.py:475
  58.8 3.7 %collective-permute-start.14 = (bf16[512,256]{1,0:T(8,128)(2,1)S(1)}, bf16[512,256]{1,0:T(8,128)(2,1)S(1)}, u32[]{:S(2)}, u32[]{:S(2)}) collective-permute-start(bf16[512,256]{1,0:T(8,128)(2,1)S(1)} %get-tuple-element.50), channel_id=1, source_target_pairs={{0,16},{1,17},{2,18},{3,19},{4,20},{5,21},{6,22},{7,23},{8,24},{9,... | collective-permute-start | bytes 786440 | tf_op jit(solution)/shard_map/ppermute | solution.py:475
  62.9 1.9 %collective-permute-start.20 = (bf16[128,1024]{1,0:T(8,128)(2,1)S(1)}, bf16[128,1024]{1,0:T(8,128)(2,1)S(1)}, u32[]{:S(2)}, u32[]{:S(2)}) collective-permute-start(bf16[128,1024]{1,0:T(8,128)(2,1)S(1)} %get-tuple-element.59), channel_id=1, source_target_pairs={{0,1},{1,2},{2,3},{3,0},{4,5},{5,6},{6,7},{7,4},{8,9},{9,10},{10,1... | collective-permute-start | bytes 786440 | tf_op jit(solution)/shard_map/ppermute | solution.py:472
  64.8 2.2 %collective-permute-start.21 = (bf16[128,1024]{1,0:T(8,128)(2,1)S(1)}, bf16[128,1024]{1,0:T(8,128)(2,1)S(1)}, u32[]{:S(2)}, u32[]{:S(2)}) collective-permute-start(bf16[128,1024]{1,0:T(8,128)(2,1)S(1)} %get-tuple-element.60), channel_id=1, source_target_pairs={{0,2},{1,3},{2,0},{3,1},{4,6},{5,7},{6,4},{7,5},{8,10},{9,11},{10,... | collective-permute-start | bytes 786440 | tf_op jit(solution)/shard_map/ppermute | solution.py:472
  67.6 2.7 %collective-permute-start.22 = (bf16[128,1024]{1,0:T(8,128)(2,1)S(1)}, bf16[128,1024]{1,0:T(8,128)(2,1)S(1)}, u32[]{:S(2)}, u32[]{:S(2)}) collective-permute-start(bf16[128,1024]{1,0:T(8,128)(2,1)S(1)} %get-tuple-element.61), channel_id=1, source_target_pairs={{0,3},{1,0},{2,1},{3,2},{4,7},{5,4},{6,5},{7,6},{8,11},{9,8},{10,9... | collective-permute-start | bytes 786440 | tf_op jit(solution)/shard_map/ppermute | solution.py:472
  70.9 2.5 %collective-permute-start.17 = (bf16[256,256]{1,0:T(8,128)(2,1)S(1)}, bf16[256,256]{1,0:T(8,128)(2,1)S(1)}, u32[]{:S(2)}, u32[]{:S(2)}) collective-permute-start(bf16[256,256]{1,0:T(8,128)(2,1)S(1)} %get-tuple-element.55), channel_id=1, source_target_pairs={{0,1},{1,2},{2,3},{3,0},{4,5},{5,6},{6,7},{7,4},{8,9},{9,10},{10,1... | collective-permute-start | bytes 393224 | tf_op jit(solution)/shard_map/ppermute | solution.py:472
  73.4 2.2 %collective-permute-start.18 = (bf16[256,256]{1,0:T(8,128)(2,1)S(1)}, bf16[256,256]{1,0:T(8,128)(2,1)S(1)}, u32[]{:S(2)}, u32[]{:S(2)}) collective-permute-start(bf16[256,256]{1,0:T(8,128)(2,1)S(1)} %get-tuple-element.56), channel_id=1, source_target_pairs={{0,2},{1,3},{2,0},{3,1},{4,6},{5,7},{6,4},{7,5},{8,10},{9,11},{10,... | collective-permute-start | bytes 393224 | tf_op jit(solution)/shard_map/ppermute | solution.py:472
  76.1 2.5 %collective-permute-done.21.refs_6_ = bf16[128,1024]{1,0:T(8,128)(2,1)S(1)} collective-permute-done((bf16[128,1024]{1,0:T(8,128)(2,1)S(1)}, bf16[128,1024]{1,0:T(8,128)(2,1)S(1)}, u32[]{:S(2)}, u32[]{:S(2)}) %collective-permute-start.21) | collective-permute-done | bytes 262176 | tf_op jit(solution)/shard_map/ppermute | solution.py:472
  78.6 1.6 %collective-permute-done.17.refs_1_ = bf16[256,256]{1,0:T(8,128)(2,1)S(1)} collective-permute-done((bf16[256,256]{1,0:T(8,128)(2,1)S(1)}, bf16[256,256]{1,0:T(8,128)(2,1)S(1)}, u32[]{:S(2)}, u32[]{:S(2)}) %collective-permute-start.17) | collective-permute-done | bytes 131104 | tf_op jit(solution)/shard_map/ppermute | solution.py:472
  (31 shorter events, 14.7 us)
Async XLA Ops:
  2.3 7.7 %collective-permute-start = (bf16[256,256]{1,0:T(8,128)(2,1)S(1)}, bf16[256,256]{1,0:T(8,128)(2,1)S(1)}, u32[]{:S(2)}, u32[]{:S(2)}) collective-permute-start(bf16[256,256]{1,0:T(8,128)(2,1)S(1)} %get-tuple-element.35), channel_id=1, source_target_pairs={{0,1},{1,2},{2,3},{3,0},{4,5},{5,6},{6,7},{7,4},{8,9},{9,10},{10,1... | collective-permute-start | bytes 393224 | tf_op jit(solution)/shard_map/ppermute | solution.py:472
  4.4 9.6 %collective-permute-start.1 = (bf16[256,256]{1,0:T(8,128)(2,1)S(1)}, bf16[256,256]{1,0:T(8,128)(2,1)S(1)}, u32[]{:S(2)}, u32[]{:S(2)}) collective-permute-start(bf16[256,256]{1,0:T(8,128)(2,1)S(1)} %get-tuple-element.36), channel_id=1, source_target_pairs={{0,2},{1,3},{2,0},{3,1},{4,6},{5,7},{6,4},{7,5},{8,10},{9,11},{10,... | collective-permute-start | bytes 393224 | tf_op jit(solution)/shard_map/ppermute | solution.py:472
  8.0 6.0 %collective-permute-start.2 = (bf16[256,256]{1,0:T(8,128)(2,1)S(1)}, bf16[256,256]{1,0:T(8,128)(2,1)S(1)}, u32[]{:S(2)}, u32[]{:S(2)}) collective-permute-start(bf16[256,256]{1,0:T(8,128)(2,1)S(1)} %get-tuple-element.37), channel_id=1, source_target_pairs={{0,3},{1,0},{2,1},{3,2},{4,7},{5,4},{6,5},{7,6},{8,11},{9,8},{10,9... | collective-permute-start | bytes 393224 | tf_op jit(solution)/shard_map/ppermute | solution.py:472
  14.0 13.2 %collective-permute-start.5 = (bf16[512,256]{1,0:T(8,128)(2,1)S(1)}, bf16[512,256]{1,0:T(8,128)(2,1)S(1)}, u32[]{:S(2)}, u32[]{:S(2)}) collective-permute-start(bf16[512,256]{1,0:T(8,128)(2,1)S(1)} %get-tuple-element.38.refs_0_.kv_ref), channel_id=1, source_target_pairs={{0,24},{1,25},{2,26},{3,27},{4,28},{5,29},{6,30},{7,31},{8,0},{9,1... | collective-permute-start | bytes 786440 | tf_op jit(solution)/shard_map/ppermute | solution.py:475
  16.9 12.3 %collective-permute-start.4 = (bf16[512,256]{1,0:T(8,128)(2,1)S(1)}, bf16[512,256]{1,0:T(8,128)(2,1)S(1)}, u32[]{:S(2)}, u32[]{:S(2)}) collective-permute-start(bf16[512,256]{1,0:T(8,128)(2,1)S(1)} %get-tuple-element.38.refs_0_.kv_ref), channel_id=1, source_target_pairs={{0,16},{1,17},{2,18},{3,19},{4,20},{5,21},{6,22},{7,23},{8,24},{9,... | collective-permute-start | bytes 786440 | tf_op jit(solution)/shard_map/ppermute | solution.py:475
  17.7 14.2 %collective-permute-start.3 = (bf16[512,256]{1,0:T(8,128)(2,1)S(1)}, bf16[512,256]{1,0:T(8,128)(2,1)S(1)}, u32[]{:S(2)}, u32[]{:S(2)}) collective-permute-start(bf16[512,256]{1,0:T(8,128)(2,1)S(1)} %get-tuple-element.38.refs_0_.kv_ref), channel_id=1, source_target_pairs={{0,8},{1,9},{2,10},{3,11},{4,12},{5,13},{6,14},{7,15},{8,16},{9,17... | collective-permute-start | bytes 786440 | tf_op jit(solution)/shard_map/ppermute | solution.py:475
  18.6 16.7 %collective-permute-start.9 = (bf16[128,1024]{1,0:T(8,128)(2,1)S(1)}, bf16[128,1024]{1,0:T(8,128)(2,1)S(1)}, u32[]{:S(2)}, u32[]{:S(2)}) collective-permute-start(bf16[128,1024]{1,0:T(8,128)(2,1)S(1)} %get-tuple-element.41), channel_id=1, source_target_pairs={{0,1},{1,2},{2,3},{3,0},{4,5},{5,6},{6,7},{7,4},{8,9},{9,10},{10,1... | collective-permute-start | bytes 786440 | tf_op jit(solution)/shard_map/ppermute | solution.py:472
  19.8 14.2 %collective-permute-start.6 = (bf16[512,256]{1,0:T(8,128)(2,1)S(1)}, bf16[512,256]{1,0:T(8,128)(2,1)S(1)}, u32[]{:S(2)}, u32[]{:S(2)}) collective-permute-start(bf16[512,256]{1,0:T(8,128)(2,1)S(1)} %get-tuple-element.39.refs_4_), channel_id=1, source_target_pairs={{0,4},{1,5},{2,6},{3,7},{4,0},{5,1},{6,2},{7,3},{8,12},{9,13},{10,... | collective-permute-start | bytes 786440 | tf_op jit(solution)/shard_map/ppermute | solution.py:478
  27.2 8.0 %collective-permute-start.10 = (bf16[128,1024]{1,0:T(8,128)(2,1)S(1)}, bf16[128,1024]{1,0:T(8,128)(2,1)S(1)}, u32[]{:S(2)}, u32[]{:S(2)}) collective-permute-start(bf16[128,1024]{1,0:T(8,128)(2,1)S(1)} %get-tuple-element.42), channel_id=1, source_target_pairs={{0,2},{1,3},{2,0},{3,1},{4,6},{5,7},{6,4},{7,5},{8,10},{9,11},{10,... | collective-permute-start | bytes 786440 | tf_op jit(solution)/shard_map/ppermute | solution.py:472
  29.2 8.7 %collective-permute-start.11 = (bf16[128,1024]{1,0:T(8,128)(2,1)S(1)}, bf16[128,1024]{1,0:T(8,128)(2,1)S(1)}, u32[]{:S(2)}, u32[]{:S(2)}) collective-permute-start(bf16[128,1024]{1,0:T(8,128)(2,1)S(1)} %get-tuple-element.43), channel_id=1, source_target_pairs={{0,3},{1,0},{2,1},{3,2},{4,7},{5,4},{6,5},{7,6},{8,11},{9,8},{10,9... | collective-permute-start | bytes 786440 | tf_op jit(solution)/shard_map/ppermute | solution.py:472
  32.3 6.0 %collective-permute-start.8 = (bf16[384,256]{1,0:T(8,128)(2,1)S(1)}, bf16[384,256]{1,0:T(8,128)(2,1)S(1)}, u32[]{:S(2)}, u32[]{:S(2)}) collective-permute-start(bf16[384,256]{1,0:T(8,128)(2,1)S(1)} %shard_map.87.e2_ref), channel_id=1, source_target_pairs={{0,4},{1,5},{2,6},{3,7},{4,0},{5,1},{6,2},{7,3},{8,12},{9,13},{10,... | collective-permute-start | bytes 589832 | tf_op jit(solution)/shard_map/ppermute | solution.py:478
  44.8 11.3 %collective-permute-start.12 = (bf16[384,256]{1,0:T(8,128)(2,1)S(1)}, bf16[384,256]{1,0:T(8,128)(2,1)S(1)}, u32[]{:S(2)}, u32[]{:S(2)}) collective-permute-start(bf16[384,256]{1,0:T(8,128)(2,1)S(1)} %get-tuple-element.47), channel_id=1, source_target_pairs={{0,4},{1,5},{2,6},{3,7},{4,0},{5,1},{6,2},{7,3},{8,12},{9,13},{10,... | collective-permute-start | bytes 589832 | tf_op jit(solution)/shard_map/ppermute | solution.py:478
  46.4 4.4 %collective-permute-start.7 = (f32[4,8,256]{2,1,0:T(8,128)S(1)}, f32[4,8,256]{2,1,0:T(8,128)S(1)}, u32[]{:S(2)}, u32[]{:S(2)}) collective-permute-start(f32[4,8,256]{2,1,0:T(8,128)S(1)} %shard_map.86.after_ref.refs_6_), channel_id=1, source_target_pairs={{0,4},{1,5},{2,6},{3,7},{4,0},{5,1},{6,2},{7,3},{8,12},{9,13},{10,... | collective-permute-start | bytes 98312 | tf_op jit(solution)/shard_map/ppermute | solution.py:478
  54.4 10.4 %collective-permute-start.16 = (bf16[128,1024]{1,0:T(8,128)(2,1)S(1)}, bf16[128,1024]{1,0:T(8,128)(2,1)S(1)}, u32[]{:S(2)}, u32[]{:S(2)}) collective-permute-start(bf16[128,1024]{1,0:T(8,128)(2,1)S(1)} %get-tuple-element.53), channel_id=1, source_target_pairs={{0,4},{1,5},{2,6},{3,7},{4,0},{5,1},{6,2},{7,3},{8,12},{9,13},{10,... | collective-permute-start | bytes 786440 | tf_op jit(solution)/shard_map/ppermute | solution.py:478
  56.5 11.0 %collective-permute-start.13 = (bf16[512,256]{1,0:T(8,128)(2,1)S(1)}, bf16[512,256]{1,0:T(8,128)(2,1)S(1)}, u32[]{:S(2)}, u32[]{:S(2)}) collective-permute-start(bf16[512,256]{1,0:T(8,128)(2,1)S(1)} %get-tuple-element.49), channel_id=1, source_target_pairs={{0,8},{1,9},{2,10},{3,11},{4,12},{5,13},{6,14},{7,15},{8,16},{9,17... | collective-permute-start | bytes 786440 | tf_op jit(solution)/shard_map/ppermute | solution.py:475
  58.8 11.6 %collective-permute-start.14 = (bf16[512,256]{1,0:T(8,128)(2,1)S(1)}, bf16[512,256]{1,0:T(8,128)(2,1)S(1)}, u32[]{:S(2)}, u32[]{:S(2)}) collective-permute-start(bf16[512,256]{1,0:T(8,128)(2,1)S(1)} %get-tuple-element.50), channel_id=1, source_target_pairs={{0,16},{1,17},{2,18},{3,19},{4,20},{5,21},{6,22},{7,23},{8,24},{9,... | collective-permute-start | bytes 786440 | tf_op jit(solution)/shard_map/ppermute | solution.py:475
  62.4 7.9 %collective-permute-start.15 = (bf16[512,256]{1,0:T(8,128)(2,1)S(1)}, bf16[512,256]{1,0:T(8,128)(2,1)S(1)}, u32[]{:S(2)}, u32[]{:S(2)}) collective-permute-start(bf16[512,256]{1,0:T(8,128)(2,1)S(1)} %get-tuple-element.51), channel_id=1, source_target_pairs={{0,24},{1,25},{2,26},{3,27},{4,28},{5,29},{6,30},{7,31},{8,0},{9,1... | collective-permute-start | bytes 786440 | tf_op jit(solution)/shard_map/ppermute | solution.py:475
  62.9 12.7 %collective-permute-start.20 = (bf16[128,1024]{1,0:T(8,128)(2,1)S(1)}, bf16[128,1024]{1,0:T(8,128)(2,1)S(1)}, u32[]{:S(2)}, u32[]{:S(2)}) collective-permute-start(bf16[128,1024]{1,0:T(8,128)(2,1)S(1)} %get-tuple-element.59), channel_id=1, source_target_pairs={{0,1},{1,2},{2,3},{3,0},{4,5},{5,6},{6,7},{7,4},{8,9},{9,10},{10,1... | collective-permute-start | bytes 786440 | tf_op jit(solution)/shard_map/ppermute | solution.py:472
  64.8 13.8 %collective-permute-start.21 = (bf16[128,1024]{1,0:T(8,128)(2,1)S(1)}, bf16[128,1024]{1,0:T(8,128)(2,1)S(1)}, u32[]{:S(2)}, u32[]{:S(2)}) collective-permute-start(bf16[128,1024]{1,0:T(8,128)(2,1)S(1)} %get-tuple-element.60), channel_id=1, source_target_pairs={{0,2},{1,3},{2,0},{3,1},{4,6},{5,7},{6,4},{7,5},{8,10},{9,11},{10,... | collective-permute-start | bytes 786440 | tf_op jit(solution)/shard_map/ppermute | solution.py:472
  67.6 11.1 %collective-permute-start.22 = (bf16[128,1024]{1,0:T(8,128)(2,1)S(1)}, bf16[128,1024]{1,0:T(8,128)(2,1)S(1)}, u32[]{:S(2)}, u32[]{:S(2)}) collective-permute-start(bf16[128,1024]{1,0:T(8,128)(2,1)S(1)} %get-tuple-element.61), channel_id=1, source_target_pairs={{0,3},{1,0},{2,1},{3,2},{4,7},{5,4},{6,5},{7,6},{8,11},{9,8},{10,9... | collective-permute-start | bytes 786440 | tf_op jit(solution)/shard_map/ppermute | solution.py:472
  70.9 9.3 %collective-permute-start.17 = (bf16[256,256]{1,0:T(8,128)(2,1)S(1)}, bf16[256,256]{1,0:T(8,128)(2,1)S(1)}, u32[]{:S(2)}, u32[]{:S(2)}) collective-permute-start(bf16[256,256]{1,0:T(8,128)(2,1)S(1)} %get-tuple-element.55), channel_id=1, source_target_pairs={{0,1},{1,2},{2,3},{3,0},{4,5},{5,6},{6,7},{7,4},{8,9},{9,10},{10,1... | collective-permute-start | bytes 393224 | tf_op jit(solution)/shard_map/ppermute | solution.py:472
  73.4 8.2 %collective-permute-start.18 = (bf16[256,256]{1,0:T(8,128)(2,1)S(1)}, bf16[256,256]{1,0:T(8,128)(2,1)S(1)}, u32[]{:S(2)}, u32[]{:S(2)}) collective-permute-start(bf16[256,256]{1,0:T(8,128)(2,1)S(1)} %get-tuple-element.56), channel_id=1, source_target_pairs={{0,2},{1,3},{2,0},{3,1},{4,6},{5,7},{6,4},{7,5},{8,10},{9,11},{10,... | collective-permute-start | bytes 393224 | tf_op jit(solution)/shard_map/ppermute | solution.py:472
  75.6 6.0 %collective-permute-start.19 = (bf16[256,256]{1,0:T(8,128)(2,1)S(1)}, bf16[256,256]{1,0:T(8,128)(2,1)S(1)}, u32[]{:S(2)}, u32[]{:S(2)}) collective-permute-start(bf16[256,256]{1,0:T(8,128)(2,1)S(1)} %get-tuple-element.57), channel_id=1, source_target_pairs={{0,3},{1,0},{2,1},{3,2},{4,7},{5,4},{6,5},{7,6},{8,11},{9,8},{10,9... | collective-permute-start | bytes 393224 | tf_op jit(solution)/shard_map/ppermute | solution.py:472
where the time goes:
time: 83.4 us; the launch traced here: 83.1 us
  starting transfers between devices  42.5 us (51%)
  waiting for transfers between devices  24.1 us (29%)
  Pallas kernels  15.9 us (19%)
    ppermute x12, starting transfers between devices, zperm(): return lax.ppermute(a, 'ctx', pairs)  24.6 us
    pallas_call x9, Pallas kernels, call(): pl.pallas_call(kernel, out_shape=tuple((jax.ShapeDtypeStruct(s, d) for s,...  15.9 us
    ppermute x12, waiting for transfers between devices, zperm(): return lax.ppermute(a, 'ctx', pairs)  13.2 us
    ppermute x6, starting transfers between devices, xperm(): lax.ppermute(a, 'ctx', [(c, (c + step * SIDES * GROUP) % devices) for c i...  10.9 us
    ppermute x5, starting transfers between devices, yperm(): return lax.ppermute(a, 'ctx', [(c, c ^ GROUP) for c in range(devices)])  6.97 us
    ppermute x6, waiting for transfers between devices, xperm(): lax.ppermute(a, 'ctx', [(c, (c + step * SIDES * GROUP) % devices) for c i...  6.54 us
    ppermute x5, waiting for transfers between devices, yperm(): return lax.ppermute(a, 'ctx', [(c, c ^ GROUP) for c in range(devices)])  4.39 us
  transfers between devices with their start and end apart: 23, of which 11 were waited for; matrix products, arithmetic and copies ran while one was open for 0% of the time, Pallas kernels for 7%

commit v1 on v0

--- a/solution.py
+++ b/solution.py
@@ -18,8 +18,9 @@
 GROUP = 4
 SIDES = 2
 XS = 4
-CHUNK = 64
+CHUNK = 128
 ROWS = REP * BLOCK
+GROWS = REP * CHUNK
 WIDE = REP * DH
 KV = 2 * DH
 PIECES = 2 * WIDE // KV
@@ -197,13 +198,13 @@
 
     def chunk(ch, carry):
         q, g = chunk_rows(slots, ranks, ch * CHUNK)
-        top = jnp.full((1, ROWS), NEG, F32)
+        top = jnp.full((1, GROWS), NEG, F32)
         for m in range(XS):
             s = dot_nt(kv_refs[m][:, :DH], q)
             sc[m * ctoks : (m + 1) * ctoks, :] = s
             top = jnp.maximum(top, jnp.max(s, axis=0, keepdims=True))
-        total = jnp.zeros((1, ROWS), F32)
-        dsum = jnp.zeros((1, ROWS), F32)
+        total = jnp.zeros((1, GROWS), F32)
+        dsum = jnp.zeros((1, GROWS), F32)
         for m in range(XS):
             w = jnp.exp2((sc[m * ctoks : (m + 1) * ctoks, :] - top) * EXP2)
             total = total + jnp.sum(w, axis=0, keepdims=True)
@@ -281,7 +282,7 @@
             out[mine, WIDE + h * DH : WIDE + (h + 1) * DH] = gqr[rows]
         return carry
 
-    lax.fori_loop(0, ctoks // BLOCK, block, 0)
+    lax.fori_loop(0, ctoks // BLOCK, block, 0, unroll=4)
     for step in range(GROUP):
         dst = lax.rem(z + step, GROUP)
         outs[step][...] = out[pl.ds(pl.multiple_of(dst * toks, toks), toks), :]
@@ -319,7 +320,7 @@
     def chunk(ch, carry):
         base = ch * CHUNK
         q, g = chunk_rows(slots, ranks, base)
-        valid = (base + lax.rem(iota((1, ROWS), 1), CHUNK) < count).astype(F32)
+        valid = (base + lax.rem(iota((1, GROWS), 1), CHUNK) < count).astype(F32)
         here, there = st_ref[ch], stp_ref[ch]
         top = jnp.maximum(here[0:1], there[0:1])
         a = jnp.exp2((here[0:1] - top) * EXP2)
@@ -327,8 +328,8 @@
         inv = 1.0 / (here[1:2] * a + there[1:2] * b)
         delta = (here[2:3] * a + there[2:3] * b) * inv
         inv = inv * valid
-        att = jnp.zeros((DH, ROWS), F32)
-        gq = jnp.zeros((DH, ROWS), F32)
+        att = jnp.zeros((DH, GROWS), F32)
+        gq = jnp.zeros((DH, GROWS), F32)
         for m in range(XS):
             p = jnp.exp2((dot_nt(kv_refs[m][:, :DH], q) - top) * EXP2) * inv
             p_high, p_low = split(p)
@@ -505,9 +506,9 @@
     e2p = yperm(e2)
     (st,) = call(
         functools.partial(stats_kernel, toks),
-        [((glob // CHUNK, 8, ROWS), F32)],
+        [((glob // CHUNK, 8, GROWS), F32)],
         (pos, *kvs, qc, qcp),
-        scratch=[((2 * GROUP * CAP, 2 * WIDE), BF16), ((XS * ctoks, ROWS), F32)],
+        scratch=[((2 * GROUP * CAP, 2 * WIDE), BF16), ((XS * ctoks, GROWS), F32)],
         moved=14 << 20,
     )
     stp = yperm(st)

time: 83.4 us -> 86.1 us (1.032)
  starting transfers between devices: 42.5 us -> 44.3 us
  Pallas kernels: 15.9 us -> 17.3 us
    ppermute x12, starting transfers between devices: 24.6 us -> 27.9 us  [zperm(): return lax.ppermute(a, 'ctx', pairs)]
    pallas_call x9, Pallas kernels: 15.9 us -> 17.3 us  [call(): pl.pallas_call(kernel, out_shape=tuple((jax.ShapeDtypeStruct(s, d) for s,...]
    ppermute x6, starting transfers between devices: 10.9 us -> 9.48 us  [xperm(): lax.ppermute(a, 'ctx', [(c, (c + step * SIDES * GROUP) % devices) for c i...]
  transfers between devices with their start and end apart: 23 -> 23, of which waited for: 11 -> 9; matrix products, arithmetic and copies ran while one was open for 0% -> 0% of each run, Pallas kernels for 7% -> 10%
where the time goes in v1:
time: 86.1 us; the launch traced here: 85.9 us
  starting transfers between devices  44.3 us (51%)
  waiting for transfers between devices  23.5 us (27%)
  Pallas kernels  17.3 us (20%)
    ppermute x12, starting transfers between devices, zperm(): return lax.ppermute(a, 'ctx', pairs)  27.9 us
    pallas_call x9, Pallas kernels, call(): pl.pallas_call(kernel, out_shape=tuple((jax.ShapeDtypeStruct(s, d) for s,...  17.3 us
    ppermute x12, waiting for transfers between devices, zperm(): return lax.ppermute(a, 'ctx', pairs)  13.1 us
    ppermute x6, starting transfers between devices, xperm(): lax.ppermute(a, 'ctx', [(c, (c + step * SIDES * GROUP) % devices) for c i...  9.48 us
    ppermute x5, starting transfers between devices, yperm(): return lax.ppermute(a, 'ctx', [(c, c ^ GROUP) for c in range(devices)])  6.99 us
    ppermute x6, waiting for transfers between devices, xperm(): lax.ppermute(a, 'ctx', [(c, (c + step * SIDES * GROUP) % devices) for c i...  6 us
    ppermute x5, waiting for transfers between devices, yperm(): return lax.ppermute(a, 'ctx', [(c, c ^ GROUP) for c in range(devices)])  4.39 us
  transfers between devices with their start and end apart: 23, of which 9 were waited for; matrix products, arithmetic and copies ran while one was open for 0% of the time, Pallas kernels for 10%

profile of v1, /device:TPU:0, one launch (start us, length us, event | category | flops | bytes accessed | tf_op | source)
XLA Modules:
  0.0 85.9 jit_solution(10023687556075623402)
XLA Ops:
  0.6 1.6 %shard_map.84 = (bf16[256,256]{1,0:T(8,128)(2,1)S(1)}, bf16[256,256]{1,0:T(8,128)(2,1)S(1)}, bf16[256,256]{1,0:T(8,128)(2,1)S(1)}, bf16[256,256]{1,0:T(8,128)(2,...) custom-call(s32[1,256]{1,0:T(1,128)} %bitcast.1, ...), custom_call_target="tpu_custom_call" | custom-call | bytes 4194304 | tf_op jit(solution)/shard_map/pallas_call | solution.py:447
  2.3 2.1 %collective-permute-start = (bf16[256,256]{1,0:T(8,128)(2,1)S(1)}, bf16[256,256]{1,0:T(8,128)(2,1)S(1)}, u32[]{:S(2)}, u32[]{:S(2)}) collective-permute-start(bf16[256,256]{1,0:T(8,128)(2,1)S(1)} %get-tuple-element.35), channel_id=1, source_target_pairs={{0,1},{1,2},{2,3},{3,0},{4,5},{5,6},{6,7},{7,4},{8,9},{9,10},{10,1... | collective-permute-start | bytes 393224 | tf_op jit(solution)/shard_map/ppermute | solution.py:473
  4.4 3.6 %collective-permute-start.1 = (bf16[256,256]{1,0:T(8,128)(2,1)S(1)}, bf16[256,256]{1,0:T(8,128)(2,1)S(1)}, u32[]{:S(2)}, u32[]{:S(2)}) collective-permute-start(bf16[256,256]{1,0:T(8,128)(2,1)S(1)} %get-tuple-element.36), channel_id=1, source_target_pairs={{0,2},{1,3},{2,0},{3,1},{4,6},{5,7},{6,4},{7,5},{8,10},{9,11},{10,... | collective-permute-start | bytes 393224 | tf_op jit(solution)/shard_map/ppermute | solution.py:473
  10.0 4.0 %collective-permute-done.1.refs_2_ = bf16[256,256]{1,0:T(8,128)(2,1)S(1)} collective-permute-done((bf16[256,256]{1,0:T(8,128)(2,1)S(1)}, bf16[256,256]{1,0:T(8,128)(2,1)S(1)}, u32[]{:S(2)}, u32[]{:S(2)}) %collective-permute-start.1) | collective-permute-done | bytes 131104 | tf_op jit(solution)/shard_map/ppermute | solution.py:473
  14.0 2.8 %collective-permute-start.5 = (bf16[512,256]{1,0:T(8,128)(2,1)S(1)}, bf16[512,256]{1,0:T(8,128)(2,1)S(1)}, u32[]{:S(2)}, u32[]{:S(2)}) collective-permute-start(bf16[512,256]{1,0:T(8,128)(2,1)S(1)} %get-tuple-element.38.refs_0_.kv_ref), channel_id=1, source_target_pairs={{0,24},{1,25},{2,26},{3,27},{4,28},{5,29},{6,30},{7,31},{8,0},{9,1... | collective-permute-start | bytes 786440 | tf_op jit(solution)/shard_map/ppermute | solution.py:476
  19.8 1.6 %collective-permute-start.6 = (bf16[512,256]{1,0:T(8,128)(2,1)S(1)}, bf16[512,256]{1,0:T(8,128)(2,1)S(1)}, u32[]{:S(2)}, u32[]{:S(2)}) collective-permute-start(bf16[512,256]{1,0:T(8,128)(2,1)S(1)} %get-tuple-element.39.refs_4_), channel_id=1, source_target_pairs={{0,4},{1,5},{2,6},{3,7},{4,0},{5,1},{6,2},{7,3},{8,12},{9,13},{10,... | collective-permute-start | bytes 786440 | tf_op jit(solution)/shard_map/ppermute | solution.py:479
  21.4 5.9 %collective-permute-done.5.refs_3_ = bf16[512,256]{1,0:T(8,128)(2,1)S(1)} collective-permute-done((bf16[512,256]{1,0:T(8,128)(2,1)S(1)}, bf16[512,256]{1,0:T(8,128)(2,1)S(1)}, u32[]{:S(2)}, u32[]{:S(2)}) %collective-permute-start.5) | collective-permute-done | bytes 262176 | tf_op jit(solution)/shard_map/ppermute | solution.py:476
  27.2 2.0 %collective-permute-start.10 = (bf16[128,1024]{1,0:T(8,128)(2,1)S(1)}, bf16[128,1024]{1,0:T(8,128)(2,1)S(1)}, u32[]{:S(2)}, u32[]{:S(2)}) collective-permute-start(bf16[128,1024]{1,0:T(8,128)(2,1)S(1)} %get-tuple-element.42), channel_id=1, source_target_pairs={{0,2},{1,3},{2,0},{3,1},{4,6},{5,7},{6,4},{7,5},{8,10},{9,11},{10,... | collective-permute-start | bytes 786440 | tf_op jit(solution)/shard_map/ppermute | solution.py:473
  29.2 2.6 %collective-permute-start.11 = (bf16[128,1024]{1,0:T(8,128)(2,1)S(1)}, bf16[128,1024]{1,0:T(8,128)(2,1)S(1)}, u32[]{:S(2)}, u32[]{:S(2)}) collective-permute-start(bf16[128,1024]{1,0:T(8,128)(2,1)S(1)} %get-tuple-element.43), channel_id=1, source_target_pairs={{0,3},{1,0},{2,1},{3,2},{4,7},{5,4},{6,5},{7,6},{8,11},{9,8},{10,9... | collective-permute-start | bytes 786440 | tf_op jit(solution)/shard_map/ppermute | solution.py:473
  32.3 1.7 %collective-permute-start.8 = (bf16[384,256]{1,0:T(8,128)(2,1)S(1)}, bf16[384,256]{1,0:T(8,128)(2,1)S(1)}, u32[]{:S(2)}, u32[]{:S(2)}) collective-permute-start(bf16[384,256]{1,0:T(8,128)(2,1)S(1)} %shard_map.87.e2_ref), channel_id=1, source_target_pairs={{0,4},{1,5},{2,6},{3,7},{4,0},{5,1},{6,2},{7,3},{8,12},{9,13},{10,... | collective-permute-start | bytes 589832 | tf_op jit(solution)/shard_map/ppermute | solution.py:479
  34.0 1.9 %shard_map.86.after_ref.refs_6_ = f32[2,8,512]{2,1,0:T(8,128)S(1)} custom-call(s32[1,256]{1,0:T(1,128)S(1)} %get-tuple-element.33.pos_ref, bf16[512,256]{1,0:T(8,128)(2,1)S(1)} %get-tuple-element.38.refs_0_.kv_ref, bf16[512,256]{1,0:T(8,128)(2,1)S(1)} %collective-permute-done.3.refs_1_, bf16[512,256]{1,0:T(8,128)(2,1)S(1)} %collective-permute-done.4.refs_2_, ...), custom_call_target="tpu_custom_call" | custom-call | bytes 14680064 | tf_op jit(solution)/shard_map/pallas_call | solution.py:447
  36.0 2.0 %collective-permute-done.11.refs_3_ = bf16[128,1024]{1,0:T(8,128)(2,1)S(1)} collective-permute-done((bf16[128,1024]{1,0:T(8,128)(2,1)S(1)}, bf16[128,1024]{1,0:T(8,128)(2,1)S(1)}, u32[]{:S(2)}, u32[]{:S(2)}) %collective-permute-start.11) | collective-permute-done | bytes 262176 | tf_op jit(solution)/shard_map/ppermute | solution.py:473
  38.3 5.4 %shard_map.88 = (bf16[128,1024]{1,0:T(8,128)(2,1)S(1)}, bf16[128,1024]{1,0:T(8,128)(2,1)S(1)}, bf16[128,1024]{1,0:T(8,128)(2,1)S(1)}, bf16[128,1024]{1,0:T(8,128...) custom-call(s32[1,256]{1,0:T(1,128)S(1)} %get-tuple-element.33.pos_ref, ...), custom_call_target="tpu_custom_call" | custom-call | bytes 41943040 | tf_op jit(solution)/shard_map/pallas_call | solution.py:447
  43.7 1.7 %collective-permute-start.12 = (bf16[384,256]{1,0:T(8,128)(2,1)S(1)}, bf16[384,256]{1,0:T(8,128)(2,1)S(1)}, u32[]{:S(2)}, u32[]{:S(2)}) collective-permute-start(bf16[384,256]{1,0:T(8,128)(2,1)S(1)} %get-tuple-element.47), channel_id=1, source_target_pairs={{0,4},{1,5},{2,6},{3,7},{4,0},{5,1},{6,2},{7,3},{8,12},{9,13},{10,... | collective-permute-start | bytes 589832 | tf_op jit(solution)/shard_map/ppermute | solution.py:479
  45.8 4.0 %collective-permute-done.7.refs_7_ = f32[2,8,512]{2,1,0:T(8,128)S(1)} collective-permute-done((f32[2,8,512]{2,1,0:T(8,128)S(1)}, f32[2,8,512]{2,1,0:T(8,128)S(1)}, u32[]{:S(2)}, u32[]{:S(2)}) %collective-permute-start.7) | collective-permute-done | bytes 32800 | tf_op jit(solution)/shard_map/ppermute | solution.py:479
  49.8 5.3 %shard_map.89 = (f32[4,512,256]{2,1,0:T(8,128)S(1)}, bf16[128,1024]{1,0:T(8,128)(2,1)S(1)}, f32[128,1024]{1,0:T(8,128)S(1)}) custom-call(s32[1,256]{1,0:T(1,128)S(1)} %get-tuple-element.33.pos_ref, bf16[512,256]{1,0:T(8,128)(2,1)S(1)} %get-tuple-element.38.refs_0_.kv_ref, bf16[512,256]{1,0:T(8,128)(2,1)S(1)} %collective-permute-done.3.refs_1_, ...), custom_call_target="tpu_custom_call" | custom-call | bytes 25165824 | tf_op jit(solution)/shard_map/pallas_call | solution.py:447
  55.1 1.7 %collective-permute-start.16 = (bf16[128,1024]{1,0:T(8,128)(2,1)S(1)}, bf16[128,1024]{1,0:T(8,128)(2,1)S(1)}, u32[]{:S(2)}, u32[]{:S(2)}) collective-permute-start(bf16[128,1024]{1,0:T(8,128)(2,1)S(1)} %get-tuple-element.53), channel_id=1, source_target_pairs={{0,4},{1,5},{2,6},{3,7},{4,0},{5,1},{6,2},{7,3},{8,12},{9,13},{10,... | collective-permute-start | bytes 786440 | tf_op jit(solution)/shard_map/ppermute | solution.py:479
  57.3 4.9 %collective-permute-start.14 = (bf16[512,256]{1,0:T(8,128)(2,1)S(1)}, bf16[512,256]{1,0:T(8,128)(2,1)S(1)}, u32[]{:S(2)}, u32[]{:S(2)}) collective-permute-start(bf16[512,256]{1,0:T(8,128)(2,1)S(1)} %get-tuple-element.50), channel_id=1, source_target_pairs={{0,16},{1,17},{2,18},{3,19},{4,20},{5,21},{6,22},{7,23},{8,24},{9,... | collective-permute-start | bytes 786440 | tf_op jit(solution)/shard_map/ppermute | solution.py:476
  62.2 1.8 %collective-permute-start.20 = (bf16[128,1024]{1,0:T(8,128)(2,1)S(1)}, bf16[128,1024]{1,0:T(8,128)(2,1)S(1)}, u32[]{:S(2)}, u32[]{:S(2)}) collective-permute-start(bf16[128,1024]{1,0:T(8,128)(2,1)S(1)} %get-tuple-element.59), channel_id=1, source_target_pairs={{0,1},{1,2},{2,3},{3,0},{4,5},{5,6},{6,7},{7,4},{8,9},{9,10},{10,1... | collective-permute-start | bytes 786440 | tf_op jit(solution)/shard_map/ppermute | solution.py:473
  64.0 2.2 %collective-permute-start.21 = (bf16[128,1024]{1,0:T(8,128)(2,1)S(1)}, bf16[128,1024]{1,0:T(8,128)(2,1)S(1)}, u32[]{:S(2)}, u32[]{:S(2)}) collective-permute-start(bf16[128,1024]{1,0:T(8,128)(2,1)S(1)} %get-tuple-element.60), channel_id=1, source_target_pairs={{0,2},{1,3},{2,0},{3,1},{4,6},{5,7},{6,4},{7,5},{8,10},{9,11},{10,... | collective-permute-start | bytes 786440 | tf_op jit(solution)/shard_map/ppermute | solution.py:473
  66.3 7.4 %collective-permute-start.22 = (bf16[128,1024]{1,0:T(8,128)(2,1)S(1)}, bf16[128,1024]{1,0:T(8,128)(2,1)S(1)}, u32[]{:S(2)}, u32[]{:S(2)}) collective-permute-start(bf16[128,1024]{1,0:T(8,128)(2,1)S(1)} %get-tuple-element.61), channel_id=1, source_target_pairs={{0,3},{1,0},{2,1},{3,2},{4,7},{5,4},{6,5},{7,6},{8,11},{9,8},{10,9... | collective-permute-start | bytes 786440 | tf_op jit(solution)/shard_map/ppermute | solution.py:473
  74.3 2.1 %collective-permute-start.18 = (bf16[256,256]{1,0:T(8,128)(2,1)S(1)}, bf16[256,256]{1,0:T(8,128)(2,1)S(1)}, u32[]{:S(2)}, u32[]{:S(2)}) collective-permute-start(bf16[256,256]{1,0:T(8,128)(2,1)S(1)} %get-tuple-element.56), channel_id=1, source_target_pairs={{0,2},{1,3},{2,0},{3,1},{4,6},{5,7},{6,4},{7,5},{8,10},{9,11},{10,... | collective-permute-start | bytes 393224 | tf_op jit(solution)/shard_map/ppermute | solution.py:473
  76.4 1.9 %collective-permute-start.19 = (bf16[256,256]{1,0:T(8,128)(2,1)S(1)}, bf16[256,256]{1,0:T(8,128)(2,1)S(1)}, u32[]{:S(2)}, u32[]{:S(2)}) collective-permute-start(bf16[256,256]{1,0:T(8,128)(2,1)S(1)} %get-tuple-element.57), channel_id=1, source_target_pairs={{0,3},{1,0},{2,1},{3,2},{4,7},{5,4},{6,5},{7,6},{8,11},{9,8},{10,9... | collective-permute-start | bytes 393224 | tf_op jit(solution)/shard_map/ppermute | solution.py:473
  78.3 4.8 %collective-permute-done.22.refs_7_ = bf16[128,1024]{1,0:T(8,128)(2,1)S(1)} collective-permute-done((bf16[128,1024]{1,0:T(8,128)(2,1)S(1)}, bf16[128,1024]{1,0:T(8,128)(2,1)S(1)}, u32[]{:S(2)}, u32[]{:S(2)}) %collective-permute-start.22) | collective-permute-done | bytes 262176 | tf_op jit(solution)/shard_map/ppermute | solution.py:473
  (31 shorter events, 10.5 us)
Async XLA Ops:
  2.3 7.7 %collective-permute-start = (bf16[256,256]{1,0:T(8,128)(2,1)S(1)}, bf16[256,256]{1,0:T(8,128)(2,1)S(1)}, u32[]{:S(2)}, u32[]{:S(2)}) collective-permute-start(bf16[256,256]{1,0:T(8,128)(2,1)S(1)} %get-tuple-element.35), channel_id=1, source_target_pairs={{0,1},{1,2},{2,3},{3,0},{4,5},{5,6},{6,7},{7,4},{8,9},{9,10},{10,1... | collective-permute-start | bytes 393224 | tf_op jit(solution)/shard_map/ppermute | solution.py:473
  4.4 9.6 %collective-permute-start.1 = (bf16[256,256]{1,0:T(8,128)(2,1)S(1)}, bf16[256,256]{1,0:T(8,128)(2,1)S(1)}, u32[]{:S(2)}, u32[]{:S(2)}) collective-permute-start(bf16[256,256]{1,0:T(8,128)(2,1)S(1)} %get-tuple-element.36), channel_id=1, source_target_pairs={{0,2},{1,3},{2,0},{3,1},{4,6},{5,7},{6,4},{7,5},{8,10},{9,11},{10,... | collective-permute-start | bytes 393224 | tf_op jit(solution)/shard_map/ppermute | solution.py:473
  8.0 6.0 %collective-permute-start.2 = (bf16[256,256]{1,0:T(8,128)(2,1)S(1)}, bf16[256,256]{1,0:T(8,128)(2,1)S(1)}, u32[]{:S(2)}, u32[]{:S(2)}) collective-permute-start(bf16[256,256]{1,0:T(8,128)(2,1)S(1)} %get-tuple-element.37), channel_id=1, source_target_pairs={{0,3},{1,0},{2,1},{3,2},{4,7},{5,4},{6,5},{7,6},{8,11},{9,8},{10,9... | collective-permute-start | bytes 393224 | tf_op jit(solution)/shard_map/ppermute | solution.py:473
  14.0 13.2 %collective-permute-start.5 = (bf16[512,256]{1,0:T(8,128)(2,1)S(1)}, bf16[512,256]{1,0:T(8,128)(2,1)S(1)}, u32[]{:S(2)}, u32[]{:S(2)}) collective-permute-start(bf16[512,256]{1,0:T(8,128)(2,1)S(1)} %get-tuple-element.38.refs_0_.kv_ref), channel_id=1, source_target_pairs={{0,24},{1,25},{2,26},{3,27},{4,28},{5,29},{6,30},{7,31},{8,0},{9,1... | collective-permute-start | bytes 786440 | tf_op jit(solution)/shard_map/ppermute | solution.py:476
  16.9 12.3 %collective-permute-start.4 = (bf16[512,256]{1,0:T(8,128)(2,1)S(1)}, bf16[512,256]{1,0:T(8,128)(2,1)S(1)}, u32[]{:S(2)}, u32[]{:S(2)}) collective-permute-start(bf16[512,256]{1,0:T(8,128)(2,1)S(1)} %get-tuple-element.38.refs_0_.kv_ref), channel_id=1, source_target_pairs={{0,16},{1,17},{2,18},{3,19},{4,20},{5,21},{6,22},{7,23},{8,24},{9,... | collective-permute-start | bytes 786440 | tf_op jit(solution)/shard_map/ppermute | solution.py:476
  17.7 14.2 %collective-permute-start.3 = (bf16[512,256]{1,0:T(8,128)(2,1)S(1)}, bf16[512,256]{1,0:T(8,128)(2,1)S(1)}, u32[]{:S(2)}, u32[]{:S(2)}) collective-permute-start(bf16[512,256]{1,0:T(8,128)(2,1)S(1)} %get-tuple-element.38.refs_0_.kv_ref), channel_id=1, source_target_pairs={{0,8},{1,9},{2,10},{3,11},{4,12},{5,13},{6,14},{7,15},{8,16},{9,17... | collective-permute-start | bytes 786440 | tf_op jit(solution)/shard_map/ppermute | solution.py:476
  18.6 17.4 %collective-permute-start.9 = (bf16[128,1024]{1,0:T(8,128)(2,1)S(1)}, bf16[128,1024]{1,0:T(8,128)(2,1)S(1)}, u32[]{:S(2)}, u32[]{:S(2)}) collective-permute-start(bf16[128,1024]{1,0:T(8,128)(2,1)S(1)} %get-tuple-element.41), channel_id=1, source_target_pairs={{0,1},{1,2},{2,3},{3,0},{4,5},{5,6},{6,7},{7,4},{8,9},{9,10},{10,1... | collective-permute-start | bytes 786440 | tf_op jit(solution)/shard_map/ppermute | solution.py:473
  19.8 14.2 %collective-permute-start.6 = (bf16[512,256]{1,0:T(8,128)(2,1)S(1)}, bf16[512,256]{1,0:T(8,128)(2,1)S(1)}, u32[]{:S(2)}, u32[]{:S(2)}) collective-permute-start(bf16[512,256]{1,0:T(8,128)(2,1)S(1)} %get-tuple-element.39.refs_4_), channel_id=1, source_target_pairs={{0,4},{1,5},{2,6},{3,7},{4,0},{5,1},{6,2},{7,3},{8,12},{9,13},{10,... | collective-permute-start | bytes 786440 | tf_op jit(solution)/shard_map/ppermute | solution.py:479
  27.2 8.7 %collective-permute-start.10 = (bf16[128,1024]{1,0:T(8,128)(2,1)S(1)}, bf16[128,1024]{1,0:T(8,128)(2,1)S(1)}, u32[]{:S(2)}, u32[]{:S(2)}) collective-permute-start(bf16[128,1024]{1,0:T(8,128)(2,1)S(1)} %get-tuple-element.42), channel_id=1, source_target_pairs={{0,2},{1,3},{2,0},{3,1},{4,6},{5,7},{6,4},{7,5},{8,10},{9,11},{10,... | collective-permute-start | bytes 786440 | tf_op jit(solution)/shard_map/ppermute | solution.py:473
  29.2 8.7 %collective-permute-start.11 = (bf16[128,1024]{1,0:T(8,128)(2,1)S(1)}, bf16[128,1024]{1,0:T(8,128)(2,1)S(1)}, u32[]{:S(2)}, u32[]{:S(2)}) collective-permute-start(bf16[128,1024]{1,0:T(8,128)(2,1)S(1)} %get-tuple-element.43), channel_id=1, source_target_pairs={{0,3},{1,0},{2,1},{3,2},{4,7},{5,4},{6,5},{7,6},{8,11},{9,8},{10,9... | collective-permute-start | bytes 786440 | tf_op jit(solution)/shard_map/ppermute | solution.py:473
  32.3 6.0 %collective-permute-start.8 = (bf16[384,256]{1,0:T(8,128)(2,1)S(1)}, bf16[384,256]{1,0:T(8,128)(2,1)S(1)}, u32[]{:S(2)}, u32[]{:S(2)}) collective-permute-start(bf16[384,256]{1,0:T(8,128)(2,1)S(1)} %shard_map.87.e2_ref), channel_id=1, source_target_pairs={{0,4},{1,5},{2,6},{3,7},{4,0},{5,1},{6,2},{7,3},{8,12},{9,13},{10,... | collective-permute-start | bytes 589832 | tf_op jit(solution)/shard_map/ppermute | solution.py:479
  43.7 13.1 %collective-permute-start.12 = (bf16[384,256]{1,0:T(8,128)(2,1)S(1)}, bf16[384,256]{1,0:T(8,128)(2,1)S(1)}, u32[]{:S(2)}, u32[]{:S(2)}) collective-permute-start(bf16[384,256]{1,0:T(8,128)(2,1)S(1)} %get-tuple-element.47), channel_id=1, source_target_pairs={{0,4},{1,5},{2,6},{3,7},{4,0},{5,1},{6,2},{7,3},{8,12},{9,13},{10,... | collective-permute-start | bytes 589832 | tf_op jit(solution)/shard_map/ppermute | solution.py:479
  45.4 4.4 %collective-permute-start.7 = (f32[2,8,512]{2,1,0:T(8,128)S(1)}, f32[2,8,512]{2,1,0:T(8,128)S(1)}, u32[]{:S(2)}, u32[]{:S(2)}) collective-permute-start(f32[2,8,512]{2,1,0:T(8,128)S(1)} %shard_map.86.after_ref.refs_6_), channel_id=1, source_target_pairs={{0,4},{1,5},{2,6},{3,7},{4,0},{5,1},{6,2},{7,3},{8,12},{9,13},{10,... | collective-permute-start | bytes 98312 | tf_op jit(solution)/shard_map/ppermute | solution.py:479
  55.1 8.8 %collective-permute-start.16 = (bf16[128,1024]{1,0:T(8,128)(2,1)S(1)}, bf16[128,1024]{1,0:T(8,128)(2,1)S(1)}, u32[]{:S(2)}, u32[]{:S(2)}) collective-permute-start(bf16[128,1024]{1,0:T(8,128)(2,1)S(1)} %get-tuple-element.53), channel_id=1, source_target_pairs={{0,4},{1,5},{2,6},{3,7},{4,0},{5,1},{6,2},{7,3},{8,12},{9,13},{10,... | collective-permute-start | bytes 786440 | tf_op jit(solution)/shard_map/ppermute | solution.py:479
  57.3 9.1 %collective-permute-start.13 = (bf16[512,256]{1,0:T(8,128)(2,1)S(1)}, bf16[512,256]{1,0:T(8,128)(2,1)S(1)}, u32[]{:S(2)}, u32[]{:S(2)}) collective-permute-start(bf16[512,256]{1,0:T(8,128)(2,1)S(1)} %get-tuple-element.49), channel_id=1, source_target_pairs={{0,8},{1,9},{2,10},{3,11},{4,12},{5,13},{6,14},{7,15},{8,16},{9,17... | collective-permute-start | bytes 786440 | tf_op jit(solution)/shard_map/ppermute | solution.py:476
  57.3 16.4 %collective-permute-start.14 = (bf16[512,256]{1,0:T(8,128)(2,1)S(1)}, bf16[512,256]{1,0:T(8,128)(2,1)S(1)}, u32[]{:S(2)}, u32[]{:S(2)}) collective-permute-start(bf16[512,256]{1,0:T(8,128)(2,1)S(1)} %get-tuple-element.50), channel_id=1, source_target_pairs={{0,16},{1,17},{2,18},{3,19},{4,20},{5,21},{6,22},{7,23},{8,24},{9,... | collective-permute-start | bytes 786440 | tf_op jit(solution)/shard_map/ppermute | solution.py:476
  62.2 11.5 %collective-permute-start.15 = (bf16[512,256]{1,0:T(8,128)(2,1)S(1)}, bf16[512,256]{1,0:T(8,128)(2,1)S(1)}, u32[]{:S(2)}, u32[]{:S(2)}) collective-permute-start(bf16[512,256]{1,0:T(8,128)(2,1)S(1)} %get-tuple-element.51), channel_id=1, source_target_pairs={{0,24},{1,25},{2,26},{3,27},{4,28},{5,29},{6,30},{7,31},{8,0},{9,1... | collective-permute-start | bytes 786440 | tf_op jit(solution)/shard_map/ppermute | solution.py:476
  62.2 14.1 %collective-permute-start.20 = (bf16[128,1024]{1,0:T(8,128)(2,1)S(1)}, bf16[128,1024]{1,0:T(8,128)(2,1)S(1)}, u32[]{:S(2)}, u32[]{:S(2)}) collective-permute-start(bf16[128,1024]{1,0:T(8,128)(2,1)S(1)} %get-tuple-element.59), channel_id=1, source_target_pairs={{0,1},{1,2},{2,3},{3,0},{4,5},{5,6},{6,7},{7,4},{8,9},{9,10},{10,1... | collective-permute-start | bytes 786440 | tf_op jit(solution)/shard_map/ppermute | solution.py:473
  64.0 14.3 %collective-permute-start.21 = (bf16[128,1024]{1,0:T(8,128)(2,1)S(1)}, bf16[128,1024]{1,0:T(8,128)(2,1)S(1)}, u32[]{:S(2)}, u32[]{:S(2)}) collective-permute-start(bf16[128,1024]{1,0:T(8,128)(2,1)S(1)} %get-tuple-element.60), channel_id=1, source_target_pairs={{0,2},{1,3},{2,0},{3,1},{4,6},{5,7},{6,4},{7,5},{8,10},{9,11},{10,... | collective-permute-start | bytes 786440 | tf_op jit(solution)/shard_map/ppermute | solution.py:473
  66.3 16.7 %collective-permute-start.22 = (bf16[128,1024]{1,0:T(8,128)(2,1)S(1)}, bf16[128,1024]{1,0:T(8,128)(2,1)S(1)}, u32[]{:S(2)}, u32[]{:S(2)}) collective-permute-start(bf16[128,1024]{1,0:T(8,128)(2,1)S(1)} %get-tuple-element.61), channel_id=1, source_target_pairs={{0,3},{1,0},{2,1},{3,2},{4,7},{5,4},{6,5},{7,6},{8,11},{9,8},{10,9... | collective-permute-start | bytes 786440 | tf_op jit(solution)/shard_map/ppermute | solution.py:473
  74.2 8.8 %collective-permute-start.17 = (bf16[256,256]{1,0:T(8,128)(2,1)S(1)}, bf16[256,256]{1,0:T(8,128)(2,1)S(1)}, u32[]{:S(2)}, u32[]{:S(2)}) collective-permute-start(bf16[256,256]{1,0:T(8,128)(2,1)S(1)} %get-tuple-element.55), channel_id=1, source_target_pairs={{0,1},{1,2},{2,3},{3,0},{4,5},{5,6},{6,7},{7,4},{8,9},{9,10},{10,1... | collective-permute-start | bytes 393224 | tf_op jit(solution)/shard_map/ppermute | solution.py:473
  74.3 8.7 %collective-permute-start.18 = (bf16[256,256]{1,0:T(8,128)(2,1)S(1)}, bf16[256,256]{1,0:T(8,128)(2,1)S(1)}, u32[]{:S(2)}, u32[]{:S(2)}) collective-permute-start(bf16[256,256]{1,0:T(8,128)(2,1)S(1)} %get-tuple-element.56), channel_id=1, source_target_pairs={{0,2},{1,3},{2,0},{3,1},{4,6},{5,7},{6,4},{7,5},{8,10},{9,11},{10,... | collective-permute-start | bytes 393224 | tf_op jit(solution)/shard_map/ppermute | solution.py:473
  76.4 8.1 %collective-permute-start.19 = (bf16[256,256]{1,0:T(8,128)(2,1)S(1)}, bf16[256,256]{1,0:T(8,128)(2,1)S(1)}, u32[]{:S(2)}, u32[]{:S(2)}) collective-permute-start(bf16[256,256]{1,0:T(8,128)(2,1)S(1)} %get-tuple-element.57), channel_id=1, source_target_pairs={{0,3},{1,0},{2,1},{3,2},{4,7},{5,4},{6,5},{7,6},{8,11},{9,8},{10,9... | collective-permute-start | bytes 393224 | tf_op jit(solution)/shard_map/ppermute | solution.py:473

commit v2 on v1

--- a/solution.py
+++ b/solution.py
@@ -24,6 +24,7 @@
 WIDE = REP * DH
 KV = 2 * DH
 PIECES = 2 * WIDE // KV
+EDGE = BLOCK // PIECES
 SCALE = 1.0 / math.sqrt(DH)
 EXP2 = SCALE * math.log2(math.e)
 NEG = -1e30
@@ -127,12 +128,14 @@
 
 def join_kernel(toks, *refs):
     zs_refs, kv_ref, qc_ref = refs[:GROUP], refs[GROUP], refs[GROUP + 1]
-    _, _, _, z = place()
+    _, _, y, z = place()
     for step in range(GROUP):
         src = lax.rem(z + GROUP - step, GROUP)
         kv_ref[pl.ds(pl.multiple_of(src * toks, toks), toks), :] = zs_refs[step][:toks, :]
         rows = PIECES * CAP
         qc_ref[pl.ds(pl.multiple_of(src * rows, rows), rows), :] = zs_refs[step][toks:, :]
+    last = slice((GROUP * toks) - BLOCK, GROUP * toks)
+    qc_ref[GROUP * PIECES * CAP :, :] = jnp.where(y == 0, kv_ref[last, :], kv_ref[:BLOCK, :])
 
 
 def side_first(x, y, m, ctoks):
@@ -151,10 +154,7 @@
         got = got + dot_nn(hot(pos_col == first + iota((glob, ctoks), 1)), kv_refs[m][...])
     out_ref[:glob, :] = got.astype(BF16)
     end = slice(ctoks - BLOCK, ctoks)
-    out_ref[glob : glob + BLOCK, :] = jnp.where(y == 0, kv_refs[0][end, :], kv_refs[1][end, :])
-    out_ref[glob + BLOCK : glob + 2 * BLOCK, :] = jnp.where(
-        y == 0, kv_refs[3][:BLOCK, :], kv_refs[0][:BLOCK, :]
-    )
+    out_ref[glob:, :] = jnp.where(y == 0, kv_refs[3][:BLOCK, :], kv_refs[1][end, :])
 
 
 def fill_slots(y, slots, mine_ref, peer_ref):
@@ -217,19 +217,21 @@
     lax.fori_loop(0, (pair_count(pos_row, x, toks) + CHUNK - 1) // CHUNK, chunk, 0)
 
 
-def near_kernel(seq, toks, pos_ref, after_ref, kv_ref, e2_ref, e2p_ref, *refs):
+def near_kernel(seq, toks, pos_ref, after_ref, kv_ref, e2_ref, e2p_ref, qcp_ref, *refs):
     qg_in = refs[:GROUP]
     outs = refs[GROUP : 2 * GROUP]
-    dw_ref, dkg_ref, e5_ref, win, dwin, kg, kgt, qg, out = refs[2 * GROUP :]
-    me, _, _, z = place()
+    dw_ref, dkg_ref, e5_ref, edge_ref, win, dwin, kg, kgt, qg, out = refs[2 * GROUP :]
+    me, _, y, z = place()
     ctoks = GROUP * toks
     pos_row = pos_ref[...]
     glob = pos_row.shape[1]
     pos_col = column(pos_row)
     first = (me // GROUP) * ctoks
-    win[:BLOCK, :] = e2p_ref[glob : glob + BLOCK, :]
+    far_edge = e2p_ref[glob:, :]
+    near_edge = qcp_ref[GROUP * PIECES * CAP :, :]
+    win[:BLOCK, :] = jnp.where(y == 0, far_edge, near_edge)
     win[BLOCK : BLOCK + ctoks, :] = kv_ref[...]
-    win[BLOCK + ctoks :, :] = e2p_ref[glob + BLOCK :, :]
+    win[BLOCK + ctoks :, :] = jnp.where(y == 0, near_edge, far_edge)
     both = (e2_ref[:glob, :].astype(F32) + e2p_ref[:glob, :].astype(F32)).astype(BF16)
     kg[...] = both
     kgt[...] = both.T
@@ -288,14 +290,15 @@
         outs[step][...] = out[pl.ds(pl.multiple_of(dst * toks, toks), toks), :]
     dw_ref[...] = dwin[BLOCK : BLOCK + ctoks, :]
     e5_ref[:glob, :] = dkg_ref[...].astype(BF16)
-    e5_ref[glob : glob + BLOCK, :] = dwin[:BLOCK, :].astype(BF16)
-    e5_ref[glob + BLOCK :, :] = dwin[BLOCK + ctoks :, :].astype(BF16)
+    low, high = dwin[:BLOCK, :], dwin[BLOCK + ctoks :, :]
+    e5_ref[glob:, :] = jnp.where(y == 0, low, high).astype(BF16)
+    edge_ref[...] = jnp.where(y == 0, high, low).astype(BF16)
 
 
 def grads_kernel(toks, pos_ref, *refs):
     kv_refs, refs = refs[:XS], refs[XS:]
-    mine_ref, peer_ref, st_ref, stp_ref, dw_ref, dkg_ref = refs[:6]
-    dkv, e4_ref, keep_ref, slots, kvt, rows_out = refs[6:]
+    mine_ref, peer_ref, st_ref, stp_ref, dw_ref, dkg_ref, edge_ref = refs[:7]
+    dkv, e4_ref, keep_ref, slots, kvt, rows_out = refs[7:]
     _, x, y, _ = place()
     ctoks = GROUP * toks
     pos_row = pos_ref[...]
@@ -358,7 +361,10 @@
         size = below(pos_row, pair_first + (side + 1) * ctoks) - before - begin
         return hot((lane == begin + slot) & (slot < size))
 
-    e4_ref[...] = dot_nn(cluster_mask(1 - y), part_high).astype(BF16)
+    half = GROUP * CAP
+    e4_ref[:half, :] = dot_nn(cluster_mask(1 - y), part_high).astype(BF16)
+    for p in range(PIECES):
+        e4_ref[half:, p * KV : (p + 1) * KV] = edge_ref[p * EDGE : (p + 1) * EDGE, :]
     mask = cluster_mask(y)
     keep_ref[...] = dot_nn(mask, part_high) + dot_nn(mask, part_low)
 
@@ -369,15 +375,13 @@
     pos_row = pos_ref[...]
     glob = pos_row.shape[1]
     far = e5p_ref[:glob, :]
-    low = e5p_ref[glob : glob + BLOCK, :].astype(F32)
-    high = e5p_ref[glob + BLOCK :, :].astype(F32)
+    edge = e5p_ref[glob:, :].astype(F32)
     at_zero = (y == 0).astype(F32)
     at_one = 1.0 - at_zero
     none = jnp.zeros((ctoks - BLOCK, KV), F32)
     edges = {
-        0: jnp.concatenate([high * at_one, none[BLOCK:], low * at_zero], axis=0),
-        1: jnp.concatenate([none, low * at_one], axis=0),
-        3: jnp.concatenate([high * at_zero, none], axis=0),
+        1: jnp.concatenate([none, edge * at_one], axis=0),
+        3: jnp.concatenate([edge * at_zero, none], axis=0),
     }
     for m in range(XS):
         first = side_first(x, y, m, ctoks)
@@ -395,13 +399,19 @@
     got_refs, refs = refs[: XS - 1], refs[XS - 1 :]
     keep_ref, e4p_ref = refs[0], refs[1]
     zs_refs, whole = refs[2 : 2 + GROUP], refs[2 + GROUP]
-    me, _, _, z = place()
+    me, _, y, z = place()
     pos_row = pos_ref[...]
     total = own_ref[...]
     for ref in got_refs:
         total = total + ref[...].astype(F32)
+    half = GROUP * CAP
+    edge = [e4p_ref[half:, p * KV : (p + 1) * KV] for p in range(PIECES)]
+    edge = jnp.concatenate(edge, axis=0).astype(F32)
+    at_zero = (y == 0).astype(F32)
+    none = jnp.zeros((GROUP * toks - 2 * BLOCK, KV), F32)
+    total = total + jnp.concatenate([edge * (1.0 - at_zero), none, edge * at_zero], axis=0)
     whole[...] = total.astype(BF16)
-    rows = (keep_ref[...] + e4p_ref[...].astype(F32)).astype(BF16)
+    rows = (keep_ref[...] + e4p_ref[:half, :].astype(F32)).astype(BF16)
     first_dev = (me // GROUP) * GROUP
     before = below(pos_row, first_dev * toks)
     slot = iota((CAP, GROUP * CAP), 0)
@@ -466,7 +476,7 @@
     part = ((toks, 2 * WIDE), BF16)
     zpart = ((zrows, KV), BF16)
     cpart = ((ctoks, KV), BF16)
-    ppart = ((glob + 2 * BLOCK, KV), BF16)
+    ppart = ((glob + BLOCK, KV), BF16)
 
     def zperm(a, step):
         pairs = [(c, c // GROUP * GROUP + (c + step) % GROUP) for c in range(devices)]
@@ -497,7 +507,7 @@
     pos = sent[2 * GROUP]
     zs = [sent[0]] + [zperm(sent[step], step) for step in range(1, GROUP)]
     kv0, qc = call(
-        functools.partial(join_kernel, toks), [cpart, ((GROUP * PIECES * CAP, KV), BF16)], tuple(zs), moved=1 << 20
+        functools.partial(join_kernel, toks), [cpart, ((GROUP * PIECES * CAP + BLOCK, KV), BF16)], tuple(zs), moved=1 << 20
     )
     kvs = [kv0] + [xperm(kv0, m) for m in range(1, XS)]
     qcp = yperm(qc)
@@ -512,10 +522,10 @@
         moved=14 << 20,
     )
     stp = yperm(st)
-    *outs, dw, dkg, e5 = call(
+    *outs, dw, dkg, e5, edge = call(
         functools.partial(near_kernel, seq, toks),
-        [part] * GROUP + [((ctoks, KV), F32), ((glob, KV), F32), ppart],
-        (pos, st, kv0, e2, e2p, *qgs),
+        [part] * GROUP + [((ctoks, KV), F32), ((glob, KV), F32), ppart, ((BLOCK, KV), BF16)],
+        (pos, st, kv0, e2, e2p, qcp, *qgs),
         scratch=[
             ((ctoks + 2 * BLOCK, KV), BF16),
             ((ctoks + 2 * BLOCK, KV), F32),
@@ -530,8 +540,8 @@
     os = [outs[0]] + [zperm(outs[step], step) for step in range(1, GROUP)]
     dkv, e4, keep = call(
         functools.partial(grads_kernel, toks),
-        [((XS, ctoks, KV), F32), ((GROUP * CAP, 2 * WIDE), BF16), ((GROUP * CAP, 2 * WIDE), F32)],
-        (pos, *kvs, qc, qcp, st, stp, dw, dkg),
+        [((XS, ctoks, KV), F32), ((GROUP * CAP + EDGE, 2 * WIDE), BF16), ((GROUP * CAP, 2 * WIDE), F32)],
+        (pos, *kvs, qc, qcp, st, stp, dw, dkg, edge),
         scratch=[
             ((2 * GROUP * CAP, 2 * WIDE), BF16),
             ((XS, KV, ctoks), BF16),

time: 86.1 us -> 83.1 us (0.965)
  waiting for transfers between devices: 23.5 us -> 21.7 us
  starting transfers between devices: 44.3 us -> 43.2 us
    ppermute x12, starting transfers between devices: 27.9 us -> 26.5 us  [zperm(): return lax.ppermute(a, 'ctx', pairs)]
    ppermute x12, waiting for transfers between devices: 13.1 us -> 12.1 us  [zperm(): return lax.ppermute(a, 'ctx', pairs)]
  transfers between devices with their start and end apart: 23 -> 23, of which waited for: 9 -> 8; matrix products, arithmetic and copies ran while one was open for 0% -> 0% of each run, Pallas kernels for 10% -> 10%
where the time goes in v2:
time: 83.1 us; the launch traced here: 83 us
  starting transfers between devices  43.2 us (52%)
  waiting for transfers between devices  21.7 us (26%)
  Pallas kernels  17.4 us (21%)
    ppermute x12, starting transfers between devices, zperm(): return lax.ppermute(a, 'ctx', pairs)  26.5 us
    pallas_call x9, Pallas kernels, call(): pl.pallas_call(kernel, out_shape=tuple((jax.ShapeDtypeStruct(s, d) for s,...  17.4 us
    ppermute x12, waiting for transfers between devices, zperm(): return lax.ppermute(a, 'ctx', pairs)  12.1 us
    ppermute x6, starting transfers between devices, xperm(): lax.ppermute(a, 'ctx', [(c, (c + step * SIDES * GROUP) % devices) for c i...  9.7 us
    ppermute x5, starting transfers between devices, yperm(): return lax.ppermute(a, 'ctx', [(c, c ^ GROUP) for c in range(devices)])  6.99 us
    ppermute x6, waiting for transfers between devices, xperm(): lax.ppermute(a, 'ctx', [(c, (c + step * SIDES * GROUP) % devices) for c i...  5.88 us
    ppermute x5, waiting for transfers between devices, yperm(): return lax.ppermute(a, 'ctx', [(c, c ^ GROUP) for c in range(devices)])  3.65 us
  transfers between devices with their start and end apart: 23, of which 8 were waited for; matrix products, arithmetic and copies ran while one was open for 0% of the time, Pallas kernels for 10%

profile of v2, /device:TPU:0, one launch (start us, length us, event | category | flops | bytes accessed | tf_op | source)
XLA Modules:
  0.0 83.0 jit_solution(369667894716296635)
XLA Ops:
  0.6 1.6 %shard_map.84 = (bf16[256,256]{1,0:T(8,128)(2,1)S(1)}, bf16[256,256]{1,0:T(8,128)(2,1)S(1)}, bf16[256,256]{1,0:T(8,128)(2,1)S(1)}, bf16[256,256]{1,0:T(8,128)(2,...) custom-call(s32[1,256]{1,0:T(1,128)} %bitcast.1, ...), custom_call_target="tpu_custom_call" | custom-call | bytes 4194304 | tf_op jit(solution)/shard_map/pallas_call | solution.py:457
  2.3 2.1 %collective-permute-start = (bf16[256,256]{1,0:T(8,128)(2,1)S(1)}, bf16[256,256]{1,0:T(8,128)(2,1)S(1)}, u32[]{:S(2)}, u32[]{:S(2)}) collective-permute-start(bf16[256,256]{1,0:T(8,128)(2,1)S(1)} %get-tuple-element.36), channel_id=1, source_target_pairs={{0,1},{1,2},{2,3},{3,0},{4,5},{5,6},{6,7},{7,4},{8,9},{9,10},{10,1... | collective-permute-start | bytes 393224 | tf_op jit(solution)/shard_map/ppermute | solution.py:483
  4.4 3.6 %collective-permute-start.1 = (bf16[256,256]{1,0:T(8,128)(2,1)S(1)}, bf16[256,256]{1,0:T(8,128)(2,1)S(1)}, u32[]{:S(2)}, u32[]{:S(2)}) collective-permute-start(bf16[256,256]{1,0:T(8,128)(2,1)S(1)} %get-tuple-element.37), channel_id=1, source_target_pairs={{0,2},{1,3},{2,0},{3,1},{4,6},{5,7},{6,4},{7,5},{8,10},{9,11},{10,... | collective-permute-start | bytes 393224 | tf_op jit(solution)/shard_map/ppermute | solution.py:483
  10.0 4.0 %collective-permute-done.1.refs_2_ = bf16[256,256]{1,0:T(8,128)(2,1)S(1)} collective-permute-done((bf16[256,256]{1,0:T(8,128)(2,1)S(1)}, bf16[256,256]{1,0:T(8,128)(2,1)S(1)}, u32[]{:S(2)}, u32[]{:S(2)}) %collective-permute-start.1) | collective-permute-done | bytes 131104 | tf_op jit(solution)/shard_map/ppermute | solution.py:483
  14.1 2.8 %collective-permute-start.5 = (bf16[512,256]{1,0:T(8,128)(2,1)S(1)}, bf16[512,256]{1,0:T(8,128)(2,1)S(1)}, u32[]{:S(2)}, u32[]{:S(2)}) collective-permute-start(bf16[512,256]{1,0:T(8,128)(2,1)S(1)} %get-tuple-element.39.refs_0_.kv_ref), channel_id=1, source_target_pairs={{0,24},{1,25},{2,26},{3,27},{4,28},{5,29},{6,30},{7,31},{8,0},{9,1... | collective-permute-start | bytes 786440 | tf_op jit(solution)/shard_map/ppermute | solution.py:486
  18.6 1.6 %collective-permute-start.6 = (bf16[576,256]{1,0:T(8,128)(2,1)S(1)}, bf16[576,256]{1,0:T(8,128)(2,1)S(1)}, u32[]{:S(2)}, u32[]{:S(2)}) collective-permute-start(bf16[576,256]{1,0:T(8,128)(2,1)S(1)} %get-tuple-element.40.refs_4_), channel_id=1, source_target_pairs={{0,4},{1,5},{2,6},{3,7},{4,0},{5,1},{6,2},{7,3},{8,12},{9,13},{10,... | collective-permute-start | bytes 884744 | tf_op jit(solution)/shard_map/ppermute | solution.py:489
  21.4 5.9 %collective-permute-done.5.refs_3_ = bf16[512,256]{1,0:T(8,128)(2,1)S(1)} collective-permute-done((bf16[512,256]{1,0:T(8,128)(2,1)S(1)}, bf16[512,256]{1,0:T(8,128)(2,1)S(1)}, u32[]{:S(2)}, u32[]{:S(2)}) %collective-permute-start.5) | collective-permute-done | bytes 262176 | tf_op jit(solution)/shard_map/ppermute | solution.py:486
  27.2 2.0 %collective-permute-start.10 = (bf16[128,1024]{1,0:T(8,128)(2,1)S(1)}, bf16[128,1024]{1,0:T(8,128)(2,1)S(1)}, u32[]{:S(2)}, u32[]{:S(2)}) collective-permute-start(bf16[128,1024]{1,0:T(8,128)(2,1)S(1)} %get-tuple-element.43), channel_id=1, source_target_pairs={{0,2},{1,3},{2,0},{3,1},{4,6},{5,7},{6,4},{7,5},{8,10},{9,11},{10,... | collective-permute-start | bytes 786440 | tf_op jit(solution)/shard_map/ppermute | solution.py:483
  29.2 2.6 %collective-permute-start.11 = (bf16[128,1024]{1,0:T(8,128)(2,1)S(1)}, bf16[128,1024]{1,0:T(8,128)(2,1)S(1)}, u32[]{:S(2)}, u32[]{:S(2)}) collective-permute-start(bf16[128,1024]{1,0:T(8,128)(2,1)S(1)} %get-tuple-element.44), channel_id=1, source_target_pairs={{0,3},{1,0},{2,1},{3,2},{4,7},{5,4},{6,5},{7,6},{8,11},{9,8},{10,9... | collective-permute-start | bytes 786440 | tf_op jit(solution)/shard_map/ppermute | solution.py:483
  32.3 1.7 %collective-permute-start.8 = (bf16[320,256]{1,0:T(8,128)(2,1)S(1)}, bf16[320,256]{1,0:T(8,128)(2,1)S(1)}, u32[]{:S(2)}, u32[]{:S(2)}) collective-permute-start(bf16[320,256]{1,0:T(8,128)(2,1)S(1)} %shard_map.87.e2_ref), channel_id=1, source_target_pairs={{0,4},{1,5},{2,6},{3,7},{4,0},{5,1},{6,2},{7,3},{8,12},{9,13},{10,... | collective-permute-start | bytes 491528 | tf_op jit(solution)/shard_map/ppermute | solution.py:489
  34.0 1.9 %shard_map.86.after_ref.refs_6_ = f32[2,8,512]{2,1,0:T(8,128)S(1)} custom-call(s32[1,256]{1,0:T(1,128)S(1)} %get-tuple-element.34.pos_ref, bf16[512,256]{1,0:T(8,128)(2,1)S(1)} %get-tuple-element.39.refs_0_.kv_ref, bf16[512,256]{1,0:T(8,128)(2,1)S(1)} %collective-permute-done.3.refs_1_, bf16[512,256]{1,0:T(8,128)(2,1)S(1)} %collective-permute-done.4.refs_2_, ...), custom_call_target="tpu_custom_call" | custom-call | bytes 14680064 | tf_op jit(solution)/shard_map/pallas_call | solution.py:457
  36.0 2.0 %collective-permute-done.11.refs_3_ = bf16[128,1024]{1,0:T(8,128)(2,1)S(1)} collective-permute-done((bf16[128,1024]{1,0:T(8,128)(2,1)S(1)}, bf16[128,1024]{1,0:T(8,128)(2,1)S(1)}, u32[]{:S(2)}, u32[]{:S(2)}) %collective-permute-start.11) | collective-permute-done | bytes 262176 | tf_op jit(solution)/shard_map/ppermute | solution.py:483
  37.9 5.5 %shard_map.88 = (bf16[128,1024]{1,0:T(8,128)(2,1)S(1)}, bf16[128,1024]{1,0:T(8,128)(2,1)S(1)}, bf16[128,1024]{1,0:T(8,128)(2,1)S(1)}, bf16[128,1024]{1,0:T(8,128...) custom-call(s32[1,256]{1,0:T(1,128)S(1)} %get-tuple-element.34.pos_r, ...), custom_call_target="tpu_custom_call" | custom-call | bytes 41943040 | tf_op jit(solution)/shard_map/pallas_call | solution.py:457
  43.4 1.7 %collective-permute-start.12 = (bf16[320,256]{1,0:T(8,128)(2,1)S(1)}, bf16[320,256]{1,0:T(8,128)(2,1)S(1)}, u32[]{:S(2)}, u32[]{:S(2)}) collective-permute-start(bf16[320,256]{1,0:T(8,128)(2,1)S(1)} %get-tuple-element.49), channel_id=1, source_target_pairs={{0,4},{1,5},{2,6},{3,7},{4,0},{5,1},{6,2},{7,3},{8,12},{9,13},{10,... | collective-permute-start | bytes 491528 | tf_op jit(solution)/shard_map/ppermute | solution.py:489
  45.5 3.6 %collective-permute-done.7.refs_7_ = f32[2,8,512]{2,1,0:T(8,128)S(1)} collective-permute-done((f32[2,8,512]{2,1,0:T(8,128)S(1)}, f32[2,8,512]{2,1,0:T(8,128)S(1)}, u32[]{:S(2)}, u32[]{:S(2)}) %collective-permute-start.7) | collective-permute-done | bytes 32800 | tf_op jit(solution)/shard_map/ppermute | solution.py:489
  49.2 5.3 %shard_map.89 = (f32[4,512,256]{2,1,0:T(8,128)S(1)}, bf16[144,1024]{1,0:T(8,128)(2,1)S(1)}, f32[128,1024]{1,0:T(8,128)S(1)}) custom-call(s32[1,256]{1,0:T(1,128)S(1)} %get-tuple-element.34.pos_ref, bf16[512,256]{1,0:T(8,128)(2,1)S(1)} %get-tuple-element.39.refs_0_.kv_ref, bf16[512,256]{1,0:T(8,128)(2,1)S(1)} %collective-permute-done.3.refs_1_, ...), custom_call_target="tpu_custom_call" | custom-call | bytes 25165824 | tf_op jit(solution)/shard_map/pallas_call | solution.py:457
  54.4 1.7 %collective-permute-start.16 = (bf16[144,1024]{1,0:T(8,128)(2,1)S(1)}, bf16[144,1024]{1,0:T(8,128)(2,1)S(1)}, u32[]{:S(2)}, u32[]{:S(2)}) collective-permute-start(bf16[144,1024]{1,0:T(8,128)(2,1)S(1)} %get-tuple-element.55), channel_id=1, source_target_pairs={{0,4},{1,5},{2,6},{3,7},{4,0},{5,1},{6,2},{7,3},{8,12},{9,13},{10,... | collective-permute-start | bytes 884744 | tf_op jit(solution)/shard_map/ppermute | solution.py:489
  56.6 5.1 %collective-permute-start.14 = (bf16[512,256]{1,0:T(8,128)(2,1)S(1)}, bf16[512,256]{1,0:T(8,128)(2,1)S(1)}, u32[]{:S(2)}, u32[]{:S(2)}) collective-permute-start(bf16[512,256]{1,0:T(8,128)(2,1)S(1)} %get-tuple-element.52), channel_id=1, source_target_pairs={{0,16},{1,17},{2,18},{3,19},{4,20},{5,21},{6,22},{7,23},{8,24},{9,... | collective-permute-start | bytes 786440 | tf_op jit(solution)/shard_map/ppermute | solution.py:486
  61.7 1.9 %collective-permute-start.20 = (bf16[128,1024]{1,0:T(8,128)(2,1)S(1)}, bf16[128,1024]{1,0:T(8,128)(2,1)S(1)}, u32[]{:S(2)}, u32[]{:S(2)}) collective-permute-start(bf16[128,1024]{1,0:T(8,128)(2,1)S(1)} %get-tuple-element.61), channel_id=1, source_target_pairs={{0,1},{1,2},{2,3},{3,0},{4,5},{5,6},{6,7},{7,4},{8,9},{9,10},{10,1... | collective-permute-start | bytes 786440 | tf_op jit(solution)/shard_map/ppermute | solution.py:483
  63.7 2.2 %collective-permute-start.21 = (bf16[128,1024]{1,0:T(8,128)(2,1)S(1)}, bf16[128,1024]{1,0:T(8,128)(2,1)S(1)}, u32[]{:S(2)}, u32[]{:S(2)}) collective-permute-start(bf16[128,1024]{1,0:T(8,128)(2,1)S(1)} %get-tuple-element.62), channel_id=1, source_target_pairs={{0,2},{1,3},{2,0},{3,1},{4,6},{5,7},{6,4},{7,5},{8,10},{9,11},{10,... | collective-permute-start | bytes 786440 | tf_op jit(solution)/shard_map/ppermute | solution.py:483
  65.9 5.9 %collective-permute-start.22 = (bf16[128,1024]{1,0:T(8,128)(2,1)S(1)}, bf16[128,1024]{1,0:T(8,128)(2,1)S(1)}, u32[]{:S(2)}, u32[]{:S(2)}) collective-permute-start(bf16[128,1024]{1,0:T(8,128)(2,1)S(1)} %get-tuple-element.63), channel_id=1, source_target_pairs={{0,3},{1,0},{2,1},{3,2},{4,7},{5,4},{6,5},{7,6},{8,11},{9,8},{10,9... | collective-permute-start | bytes 786440 | tf_op jit(solution)/shard_map/ppermute | solution.py:483
  72.4 2.1 %collective-permute-start.18 = (bf16[256,256]{1,0:T(8,128)(2,1)S(1)}, bf16[256,256]{1,0:T(8,128)(2,1)S(1)}, u32[]{:S(2)}, u32[]{:S(2)}) collective-permute-start(bf16[256,256]{1,0:T(8,128)(2,1)S(1)} %get-tuple-element.58), channel_id=1, source_target_pairs={{0,2},{1,3},{2,0},{3,1},{4,6},{5,7},{6,4},{7,5},{8,10},{9,11},{10,... | collective-permute-start | bytes 393224 | tf_op jit(solution)/shard_map/ppermute | solution.py:483
  74.5 1.8 %collective-permute-start.19 = (bf16[256,256]{1,0:T(8,128)(2,1)S(1)}, bf16[256,256]{1,0:T(8,128)(2,1)S(1)}, u32[]{:S(2)}, u32[]{:S(2)}) collective-permute-start(bf16[256,256]{1,0:T(8,128)(2,1)S(1)} %get-tuple-element.59), channel_id=1, source_target_pairs={{0,3},{1,0},{2,1},{3,2},{4,7},{5,4},{6,5},{7,6},{8,11},{9,8},{10,9... | collective-permute-start | bytes 393224 | tf_op jit(solution)/shard_map/ppermute | solution.py:483
  76.3 3.3 %collective-permute-done.22.refs_7_ = bf16[128,1024]{1,0:T(8,128)(2,1)S(1)} collective-permute-done((bf16[128,1024]{1,0:T(8,128)(2,1)S(1)}, bf16[128,1024]{1,0:T(8,128)(2,1)S(1)}, u32[]{:S(2)}, u32[]{:S(2)}) %collective-permute-start.22) | collective-permute-done | bytes 262176 | tf_op jit(solution)/shard_map/ppermute | solution.py:483
  (31 shorter events, 10.5 us)
Async XLA Ops:
  2.3 7.7 %collective-permute-start = (bf16[256,256]{1,0:T(8,128)(2,1)S(1)}, bf16[256,256]{1,0:T(8,128)(2,1)S(1)}, u32[]{:S(2)}, u32[]{:S(2)}) collective-permute-start(bf16[256,256]{1,0:T(8,128)(2,1)S(1)} %get-tuple-element.36), channel_id=1, source_target_pairs={{0,1},{1,2},{2,3},{3,0},{4,5},{5,6},{6,7},{7,4},{8,9},{9,10},{10,1... | collective-permute-start | bytes 393224 | tf_op jit(solution)/shard_map/ppermute | solution.py:483
  4.4 9.6 %collective-permute-start.1 = (bf16[256,256]{1,0:T(8,128)(2,1)S(1)}, bf16[256,256]{1,0:T(8,128)(2,1)S(1)}, u32[]{:S(2)}, u32[]{:S(2)}) collective-permute-start(bf16[256,256]{1,0:T(8,128)(2,1)S(1)} %get-tuple-element.37), channel_id=1, source_target_pairs={{0,2},{1,3},{2,0},{3,1},{4,6},{5,7},{6,4},{7,5},{8,10},{9,11},{10,... | collective-permute-start | bytes 393224 | tf_op jit(solution)/shard_map/ppermute | solution.py:483
  8.0 6.0 %collective-permute-start.2 = (bf16[256,256]{1,0:T(8,128)(2,1)S(1)}, bf16[256,256]{1,0:T(8,128)(2,1)S(1)}, u32[]{:S(2)}, u32[]{:S(2)}) collective-permute-start(bf16[256,256]{1,0:T(8,128)(2,1)S(1)} %get-tuple-element.38), channel_id=1, source_target_pairs={{0,3},{1,0},{2,1},{3,2},{4,7},{5,4},{6,5},{7,6},{8,11},{9,8},{10,9... | collective-permute-start | bytes 393224 | tf_op jit(solution)/shard_map/ppermute | solution.py:483
  14.1 13.2 %collective-permute-start.5 = (bf16[512,256]{1,0:T(8,128)(2,1)S(1)}, bf16[512,256]{1,0:T(8,128)(2,1)S(1)}, u32[]{:S(2)}, u32[]{:S(2)}) collective-permute-start(bf16[512,256]{1,0:T(8,128)(2,1)S(1)} %get-tuple-element.39.refs_0_.kv_ref), channel_id=1, source_target_pairs={{0,24},{1,25},{2,26},{3,27},{4,28},{5,29},{6,30},{7,31},{8,0},{9,1... | collective-permute-start | bytes 786440 | tf_op jit(solution)/shard_map/ppermute | solution.py:486
  16.9 12.3 %collective-permute-start.4 = (bf16[512,256]{1,0:T(8,128)(2,1)S(1)}, bf16[512,256]{1,0:T(8,128)(2,1)S(1)}, u32[]{:S(2)}, u32[]{:S(2)}) collective-permute-start(bf16[512,256]{1,0:T(8,128)(2,1)S(1)} %get-tuple-element.39.refs_0_.kv_ref), channel_id=1, source_target_pairs={{0,16},{1,17},{2,18},{3,19},{4,20},{5,21},{6,22},{7,23},{8,24},{9,... | collective-permute-start | bytes 786440 | tf_op jit(solution)/shard_map/ppermute | solution.py:486
  17.7 14.2 %collective-permute-start.3 = (bf16[512,256]{1,0:T(8,128)(2,1)S(1)}, bf16[512,256]{1,0:T(8,128)(2,1)S(1)}, u32[]{:S(2)}, u32[]{:S(2)}) collective-permute-start(bf16[512,256]{1,0:T(8,128)(2,1)S(1)} %get-tuple-element.39.refs_0_.kv_ref), channel_id=1, source_target_pairs={{0,8},{1,9},{2,10},{3,11},{4,12},{5,13},{6,14},{7,15},{8,16},{9,17... | collective-permute-start | bytes 786440 | tf_op jit(solution)/shard_map/ppermute | solution.py:486
  18.6 15.4 %collective-permute-start.6 = (bf16[576,256]{1,0:T(8,128)(2,1)S(1)}, bf16[576,256]{1,0:T(8,128)(2,1)S(1)}, u32[]{:S(2)}, u32[]{:S(2)}) collective-permute-start(bf16[576,256]{1,0:T(8,128)(2,1)S(1)} %get-tuple-element.40.refs_4_), channel_id=1, source_target_pairs={{0,4},{1,5},{2,6},{3,7},{4,0},{5,1},{6,2},{7,3},{8,12},{9,13},{10,... | collective-permute-start | bytes 884744 | tf_op jit(solution)/shard_map/ppermute | solution.py:489
  20.1 15.8 %collective-permute-start.9 = (bf16[128,1024]{1,0:T(8,128)(2,1)S(1)}, bf16[128,1024]{1,0:T(8,128)(2,1)S(1)}, u32[]{:S(2)}, u32[]{:S(2)}) collective-permute-start(bf16[128,1024]{1,0:T(8,128)(2,1)S(1)} %get-tuple-element.42), channel_id=1, source_target_pairs={{0,1},{1,2},{2,3},{3,0},{4,5},{5,6},{6,7},{7,4},{8,9},{9,10},{10,1... | collective-permute-start | bytes 786440 | tf_op jit(solution)/shard_map/ppermute | solution.py:483
  27.2 8.7 %collective-permute-start.10 = (bf16[128,1024]{1,0:T(8,128)(2,1)S(1)}, bf16[128,1024]{1,0:T(8,128)(2,1)S(1)}, u32[]{:S(2)}, u32[]{:S(2)}) collective-permute-start(bf16[128,1024]{1,0:T(8,128)(2,1)S(1)} %get-tuple-element.43), channel_id=1, source_target_pairs={{0,2},{1,3},{2,0},{3,1},{4,6},{5,7},{6,4},{7,5},{8,10},{9,11},{10,... | collective-permute-start | bytes 786440 | tf_op jit(solution)/shard_map/ppermute | solution.py:483
  29.2 8.7 %collective-permute-start.11 = (bf16[128,1024]{1,0:T(8,128)(2,1)S(1)}, bf16[128,1024]{1,0:T(8,128)(2,1)S(1)}, u32[]{:S(2)}, u32[]{:S(2)}) collective-permute-start(bf16[128,1024]{1,0:T(8,128)(2,1)S(1)} %get-tuple-element.44), channel_id=1, source_target_pairs={{0,3},{1,0},{2,1},{3,2},{4,7},{5,4},{6,5},{7,6},{8,11},{9,8},{10,9... | collective-permute-start | bytes 786440 | tf_op jit(solution)/shard_map/ppermute | solution.py:483
  32.3 5.6 %collective-permute-start.8 = (bf16[320,256]{1,0:T(8,128)(2,1)S(1)}, bf16[320,256]{1,0:T(8,128)(2,1)S(1)}, u32[]{:S(2)}, u32[]{:S(2)}) collective-permute-start(bf16[320,256]{1,0:T(8,128)(2,1)S(1)} %shard_map.87.e2_ref), channel_id=1, source_target_pairs={{0,4},{1,5},{2,6},{3,7},{4,0},{5,1},{6,2},{7,3},{8,12},{9,13},{10,... | collective-permute-start | bytes 491528 | tf_op jit(solution)/shard_map/ppermute | solution.py:489
  43.4 12.7 %collective-permute-start.12 = (bf16[320,256]{1,0:T(8,128)(2,1)S(1)}, bf16[320,256]{1,0:T(8,128)(2,1)S(1)}, u32[]{:S(2)}, u32[]{:S(2)}) collective-permute-start(bf16[320,256]{1,0:T(8,128)(2,1)S(1)} %get-tuple-element.49), channel_id=1, source_target_pairs={{0,4},{1,5},{2,6},{3,7},{4,0},{5,1},{6,2},{7,3},{8,12},{9,13},{10,... | collective-permute-start | bytes 491528 | tf_op jit(solution)/shard_map/ppermute | solution.py:489
  45.1 4.1 %collective-permute-start.7 = (f32[2,8,512]{2,1,0:T(8,128)S(1)}, f32[2,8,512]{2,1,0:T(8,128)S(1)}, u32[]{:S(2)}, u32[]{:S(2)}) collective-permute-start(f32[2,8,512]{2,1,0:T(8,128)S(1)} %shard_map.86.after_ref.refs_6_), channel_id=1, source_target_pairs={{0,4},{1,5},{2,6},{3,7},{4,0},{5,1},{6,2},{7,3},{8,12},{9,13},{10,... | collective-permute-start | bytes 98312 | tf_op jit(solution)/shard_map/ppermute | solution.py:489
  54.4 9.2 %collective-permute-start.16 = (bf16[144,1024]{1,0:T(8,128)(2,1)S(1)}, bf16[144,1024]{1,0:T(8,128)(2,1)S(1)}, u32[]{:S(2)}, u32[]{:S(2)}) collective-permute-start(bf16[144,1024]{1,0:T(8,128)(2,1)S(1)} %get-tuple-element.55), channel_id=1, source_target_pairs={{0,4},{1,5},{2,6},{3,7},{4,0},{5,1},{6,2},{7,3},{8,12},{9,13},{10,... | collective-permute-start | bytes 884744 | tf_op jit(solution)/shard_map/ppermute | solution.py:489
  56.5 9.3 %collective-permute-start.13 = (bf16[512,256]{1,0:T(8,128)(2,1)S(1)}, bf16[512,256]{1,0:T(8,128)(2,1)S(1)}, u32[]{:S(2)}, u32[]{:S(2)}) collective-permute-start(bf16[512,256]{1,0:T(8,128)(2,1)S(1)} %get-tuple-element.51), channel_id=1, source_target_pairs={{0,8},{1,9},{2,10},{3,11},{4,12},{5,13},{6,14},{7,15},{8,16},{9,17... | collective-permute-start | bytes 786440 | tf_op jit(solution)/shard_map/ppermute | solution.py:486
  56.6 15.1 %collective-permute-start.14 = (bf16[512,256]{1,0:T(8,128)(2,1)S(1)}, bf16[512,256]{1,0:T(8,128)(2,1)S(1)}, u32[]{:S(2)}, u32[]{:S(2)}) collective-permute-start(bf16[512,256]{1,0:T(8,128)(2,1)S(1)} %get-tuple-element.52), channel_id=1, source_target_pairs={{0,16},{1,17},{2,18},{3,19},{4,20},{5,21},{6,22},{7,23},{8,24},{9,... | collective-permute-start | bytes 786440 | tf_op jit(solution)/shard_map/ppermute | solution.py:486
  61.7 10.0 %collective-permute-start.15 = (bf16[512,256]{1,0:T(8,128)(2,1)S(1)}, bf16[512,256]{1,0:T(8,128)(2,1)S(1)}, u32[]{:S(2)}, u32[]{:S(2)}) collective-permute-start(bf16[512,256]{1,0:T(8,128)(2,1)S(1)} %get-tuple-element.53), channel_id=1, source_target_pairs={{0,24},{1,25},{2,26},{3,27},{4,28},{5,29},{6,30},{7,31},{8,0},{9,1... | collective-permute-start | bytes 786440 | tf_op jit(solution)/shard_map/ppermute | solution.py:486
  61.7 12.7 %collective-permute-start.20 = (bf16[128,1024]{1,0:T(8,128)(2,1)S(1)}, bf16[128,1024]{1,0:T(8,128)(2,1)S(1)}, u32[]{:S(2)}, u32[]{:S(2)}) collective-permute-start(bf16[128,1024]{1,0:T(8,128)(2,1)S(1)} %get-tuple-element.61), channel_id=1, source_target_pairs={{0,1},{1,2},{2,3},{3,0},{4,5},{5,6},{6,7},{7,4},{8,9},{9,10},{10,1... | collective-permute-start | bytes 786440 | tf_op jit(solution)/shard_map/ppermute | solution.py:483
  63.7 12.6 %collective-permute-start.21 = (bf16[128,1024]{1,0:T(8,128)(2,1)S(1)}, bf16[128,1024]{1,0:T(8,128)(2,1)S(1)}, u32[]{:S(2)}, u32[]{:S(2)}) collective-permute-start(bf16[128,1024]{1,0:T(8,128)(2,1)S(1)} %get-tuple-element.62), channel_id=1, source_target_pairs={{0,2},{1,3},{2,0},{3,1},{4,6},{5,7},{6,4},{7,5},{8,10},{9,11},{10,... | collective-permute-start | bytes 786440 | tf_op jit(solution)/shard_map/ppermute | solution.py:483
  65.9 13.7 %collective-permute-start.22 = (bf16[128,1024]{1,0:T(8,128)(2,1)S(1)}, bf16[128,1024]{1,0:T(8,128)(2,1)S(1)}, u32[]{:S(2)}, u32[]{:S(2)}) collective-permute-start(bf16[128,1024]{1,0:T(8,128)(2,1)S(1)} %get-tuple-element.63), channel_id=1, source_target_pairs={{0,3},{1,0},{2,1},{3,2},{4,7},{5,4},{6,5},{7,6},{8,11},{9,8},{10,9... | collective-permute-start | bytes 786440 | tf_op jit(solution)/shard_map/ppermute | solution.py:483
  72.3 7.7 %collective-permute-start.17 = (bf16[256,256]{1,0:T(8,128)(2,1)S(1)}, bf16[256,256]{1,0:T(8,128)(2,1)S(1)}, u32[]{:S(2)}, u32[]{:S(2)}) collective-permute-start(bf16[256,256]{1,0:T(8,128)(2,1)S(1)} %get-tuple-element.57), channel_id=1, source_target_pairs={{0,1},{1,2},{2,3},{3,0},{4,5},{5,6},{6,7},{7,4},{8,9},{9,10},{10,1... | collective-permute-start | bytes 393224 | tf_op jit(solution)/shard_map/ppermute | solution.py:483
  72.4 7.6 %collective-permute-start.18 = (bf16[256,256]{1,0:T(8,128)(2,1)S(1)}, bf16[256,256]{1,0:T(8,128)(2,1)S(1)}, u32[]{:S(2)}, u32[]{:S(2)}) collective-permute-start(bf16[256,256]{1,0:T(8,128)(2,1)S(1)} %get-tuple-element.58), channel_id=1, source_target_pairs={{0,2},{1,3},{2,0},{3,1},{4,6},{5,7},{6,4},{7,5},{8,10},{9,11},{10,... | collective-permute-start | bytes 393224 | tf_op jit(solution)/shard_map/ppermute | solution.py:483
  74.5 7.0 %collective-permute-start.19 = (bf16[256,256]{1,0:T(8,128)(2,1)S(1)}, bf16[256,256]{1,0:T(8,128)(2,1)S(1)}, u32[]{:S(2)}, u32[]{:S(2)}) collective-permute-start(bf16[256,256]{1,0:T(8,128)(2,1)S(1)} %get-tuple-element.59), channel_id=1, source_target_pairs={{0,3},{1,0},{2,1},{3,2},{4,7},{5,4},{6,5},{7,6},{8,11},{9,8},{10,9... | collective-permute-start | bytes 393224 | tf_op jit(solution)/shard_map/ppermute | solution.py:483

commit v3 on v2

--- a/solution.py
+++ b/solution.py
@@ -297,12 +297,11 @@
 
 def grads_kernel(toks, pos_ref, *refs):
     kv_refs, refs = refs[:XS], refs[XS:]
-    mine_ref, peer_ref, st_ref, stp_ref, dw_ref, dkg_ref, edge_ref = refs[:7]
-    dkv, e4_ref, keep_ref, slots, kvt, rows_out = refs[7:]
+    mine_ref, peer_ref, st_ref, stp_ref, dw_ref, edge_ref = refs[:6]
+    dkv, e4_ref, keep_ref, slots, kvt, rows_out = refs[6:]
     _, x, y, _ = place()
     ctoks = GROUP * toks
     pos_row = pos_ref[...]
-    glob = pos_row.shape[1]
     pos_col = column(pos_row)
     pair_first = x * (SIDES * ctoks)
     before = below(pos_row, pair_first)
@@ -313,12 +312,9 @@
     for m in range(XS):
         kvt[m] = kv_refs[m][...].T
 
-    far_high, far_low = split(dkg_ref[...])
-    for m in range(XS):
-        first = side_first(x, y, m, ctoks)
-        mask = hot(first + iota((ctoks, glob), 0) == pos_row)
-        whole = dot_nn(mask, far_high) + dot_nn(mask, far_low)
-        dkv[m] = whole + dw_ref[...] if m == 0 else whole
+    dkv[0] = dw_ref[...]
+    for m in range(1, XS):
+        dkv[m] = jnp.zeros((ctoks, KV), F32)
 
     def chunk(ch, carry):
         base = ch * CHUNK
@@ -369,12 +365,12 @@
     keep_ref[...] = dot_nn(mask, part_high) + dot_nn(mask, part_low)
 
 
-def peer_kernel(toks, pos_ref, dkv_ref, e5p_ref, own_ref, *send_refs):
+def peer_kernel(toks, pos_ref, dkv_ref, dkg_ref, e5p_ref, own_ref, *send_refs):
     _, x, y, _ = place()
     ctoks = GROUP * toks
     pos_row = pos_ref[...]
     glob = pos_row.shape[1]
-    far = e5p_ref[:glob, :]
+    far_high, far_low = split(dkg_ref[...] + e5p_ref[:glob, :].astype(F32))
     edge = e5p_ref[glob:, :].astype(F32)
     at_zero = (y == 0).astype(F32)
     at_one = 1.0 - at_zero
@@ -386,7 +382,7 @@
     for m in range(XS):
         first = side_first(x, y, m, ctoks)
         mask = hot(first + iota((ctoks, glob), 0) == pos_row)
-        whole = dkv_ref[m] + dot_nn(mask, far)
+        whole = dkv_ref[m] + dot_nn(mask, far_high) + dot_nn(mask, far_low)
         if m in edges:
             whole = whole + edges[m]
         if m == 0:
@@ -541,7 +537,7 @@
     dkv, e4, keep = call(
         functools.partial(grads_kernel, toks),
         [((XS, ctoks, KV), F32), ((GROUP * CAP + EDGE, 2 * WIDE), BF16), ((GROUP * CAP, 2 * WIDE), F32)],
-        (pos, *kvs, qc, qcp, st, stp, dw, dkg, edge),
+        (pos, *kvs, qc, qcp, st, stp, dw, edge),
         scratch=[
             ((2 * GROUP * CAP, 2 * WIDE), BF16),
             ((XS, KV, ctoks), BF16),
@@ -552,7 +548,7 @@
     own, *sends = call(
         functools.partial(peer_kernel, toks),
         [((ctoks, KV), F32)] + [cpart] * (XS - 1),
-        (pos, dkv, e5p),
+        (pos, dkv, dkg, e5p),
         moved=3 << 20,
     )
     got = [xperm(sends[m - 1], m) for m in range(1, XS)]

time: 83.1 us -> 83.1 us (level)
  no operation moved by 1% of the time
where the time goes in v3:
time: 83.1 us; the launch traced here: 82.9 us
  starting transfers between devices  43.2 us (52%)
  waiting for transfers between devices  21.7 us (26%)
  Pallas kernels  17.3 us (21%)
    ppermute x12, starting transfers between devices, zperm(): return lax.ppermute(a, 'ctx', pairs)  26.5 us
    pallas_call x9, Pallas kernels, call(): pl.pallas_call(kernel, out_shape=tuple((jax.ShapeDtypeStruct(s, d) for s,...  17.3 us
    ppermute x12, waiting for transfers between devices, zperm(): return lax.ppermute(a, 'ctx', pairs)  12.2 us
    ppermute x6, starting transfers between devices, xperm(): lax.ppermute(a, 'ctx', [(c, (c + step * SIDES * GROUP) % devices) for c i...  9.7 us
    ppermute x5, starting transfers between devices, yperm(): return lax.ppermute(a, 'ctx', [(c, c ^ GROUP) for c in range(devices)])  6.99 us
    ppermute x6, waiting for transfers between devices, xperm(): lax.ppermute(a, 'ctx', [(c, (c + step * SIDES * GROUP) % devices) for c i...  5.88 us
    ppermute x5, waiting for transfers between devices, yperm(): return lax.ppermute(a, 'ctx', [(c, c ^ GROUP) for c in range(devices)])  3.65 us
  transfers between devices with their start and end apart: 23, of which 8 were waited for; matrix products, arithmetic and copies ran while one was open for 0% of the time, Pallas kernels for 10%

profile of v3, /device:TPU:0, one launch (start us, length us, event | category | flops | bytes accessed | tf_op | source)
XLA Modules:
  0.0 82.9 jit_solution(14065082983882585528)
XLA Ops:
  0.6 1.6 %shard_map.84 = (bf16[256,256]{1,0:T(8,128)(2,1)S(1)}, bf16[256,256]{1,0:T(8,128)(2,1)S(1)}, bf16[256,256]{1,0:T(8,128)(2,1)S(1)}, bf16[256,256]{1,0:T(8,128)(2,...) custom-call(s32[1,256]{1,0:T(1,128)} %bitcast.1, ...), custom_call_target="tpu_custom_call" | custom-call | bytes 4194304 | tf_op jit(solution)/shard_map/pallas_call | solution.py:453
  2.3 2.1 %collective-permute-start = (bf16[256,256]{1,0:T(8,128)(2,1)S(1)}, bf16[256,256]{1,0:T(8,128)(2,1)S(1)}, u32[]{:S(2)}, u32[]{:S(2)}) collective-permute-start(bf16[256,256]{1,0:T(8,128)(2,1)S(1)} %get-tuple-element.36), channel_id=1, source_target_pairs={{0,1},{1,2},{2,3},{3,0},{4,5},{5,6},{6,7},{7,4},{8,9},{9,10},{10,1... | collective-permute-start | bytes 393224 | tf_op jit(solution)/shard_map/ppermute | solution.py:479
  4.4 3.6 %collective-permute-start.1 = (bf16[256,256]{1,0:T(8,128)(2,1)S(1)}, bf16[256,256]{1,0:T(8,128)(2,1)S(1)}, u32[]{:S(2)}, u32[]{:S(2)}) collective-permute-start(bf16[256,256]{1,0:T(8,128)(2,1)S(1)} %get-tuple-element.37), channel_id=1, source_target_pairs={{0,2},{1,3},{2,0},{3,1},{4,6},{5,7},{6,4},{7,5},{8,10},{9,11},{10,... | collective-permute-start | bytes 393224 | tf_op jit(solution)/shard_map/ppermute | solution.py:479
  10.0 4.0 %collective-permute-done.1.refs_2_ = bf16[256,256]{1,0:T(8,128)(2,1)S(1)} collective-permute-done((bf16[256,256]{1,0:T(8,128)(2,1)S(1)}, bf16[256,256]{1,0:T(8,128)(2,1)S(1)}, u32[]{:S(2)}, u32[]{:S(2)}) %collective-permute-start.1) | collective-permute-done | bytes 131104 | tf_op jit(solution)/shard_map/ppermute | solution.py:479
  14.0 2.8 %collective-permute-start.5 = (bf16[512,256]{1,0:T(8,128)(2,1)S(1)}, bf16[512,256]{1,0:T(8,128)(2,1)S(1)}, u32[]{:S(2)}, u32[]{:S(2)}) collective-permute-start(bf16[512,256]{1,0:T(8,128)(2,1)S(1)} %get-tuple-element.39.refs_0_.kv_ref), channel_id=1, source_target_pairs={{0,24},{1,25},{2,26},{3,27},{4,28},{5,29},{6,30},{7,31},{8,0},{9,1... | collective-permute-start | bytes 786440 | tf_op jit(solution)/shard_map/ppermute | solution.py:482
  18.6 1.6 %collective-permute-start.6 = (bf16[576,256]{1,0:T(8,128)(2,1)S(1)}, bf16[576,256]{1,0:T(8,128)(2,1)S(1)}, u32[]{:S(2)}, u32[]{:S(2)}) collective-permute-start(bf16[576,256]{1,0:T(8,128)(2,1)S(1)} %get-tuple-element.40.refs_4_), channel_id=1, source_target_pairs={{0,4},{1,5},{2,6},{3,7},{4,0},{5,1},{6,2},{7,3},{8,12},{9,13},{10,... | collective-permute-start | bytes 884744 | tf_op jit(solution)/shard_map/ppermute | solution.py:485
  21.4 5.9 %collective-permute-done.5.refs_3_ = bf16[512,256]{1,0:T(8,128)(2,1)S(1)} collective-permute-done((bf16[512,256]{1,0:T(8,128)(2,1)S(1)}, bf16[512,256]{1,0:T(8,128)(2,1)S(1)}, u32[]{:S(2)}, u32[]{:S(2)}) %collective-permute-start.5) | collective-permute-done | bytes 262176 | tf_op jit(solution)/shard_map/ppermute | solution.py:482
  27.2 2.0 %collective-permute-start.10 = (bf16[128,1024]{1,0:T(8,128)(2,1)S(1)}, bf16[128,1024]{1,0:T(8,128)(2,1)S(1)}, u32[]{:S(2)}, u32[]{:S(2)}) collective-permute-start(bf16[128,1024]{1,0:T(8,128)(2,1)S(1)} %get-tuple-element.43), channel_id=1, source_target_pairs={{0,2},{1,3},{2,0},{3,1},{4,6},{5,7},{6,4},{7,5},{8,10},{9,11},{10,... | collective-permute-start | bytes 786440 | tf_op jit(solution)/shard_map/ppermute | solution.py:479
  29.2 2.6 %collective-permute-start.11 = (bf16[128,1024]{1,0:T(8,128)(2,1)S(1)}, bf16[128,1024]{1,0:T(8,128)(2,1)S(1)}, u32[]{:S(2)}, u32[]{:S(2)}) collective-permute-start(bf16[128,1024]{1,0:T(8,128)(2,1)S(1)} %get-tuple-element.44), channel_id=1, source_target_pairs={{0,3},{1,0},{2,1},{3,2},{4,7},{5,4},{6,5},{7,6},{8,11},{9,8},{10,9... | collective-permute-start | bytes 786440 | tf_op jit(solution)/shard_map/ppermute | solution.py:479
  32.3 1.7 %collective-permute-start.8 = (bf16[320,256]{1,0:T(8,128)(2,1)S(1)}, bf16[320,256]{1,0:T(8,128)(2,1)S(1)}, u32[]{:S(2)}, u32[]{:S(2)}) collective-permute-start(bf16[320,256]{1,0:T(8,128)(2,1)S(1)} %shard_map.87.e2_ref), channel_id=1, source_target_pairs={{0,4},{1,5},{2,6},{3,7},{4,0},{5,1},{6,2},{7,3},{8,12},{9,13},{10,... | collective-permute-start | bytes 491528 | tf_op jit(solution)/shard_map/ppermute | solution.py:485
  34.0 1.9 %shard_map.86.after_ref.refs_6_ = f32[2,8,512]{2,1,0:T(8,128)S(1)} custom-call(s32[1,256]{1,0:T(1,128)S(1)} %get-tuple-element.34.pos_ref, bf16[512,256]{1,0:T(8,128)(2,1)S(1)} %get-tuple-element.39.refs_0_.kv_ref, bf16[512,256]{1,0:T(8,128)(2,1)S(1)} %collective-permute-done.3.refs_1_, bf16[512,256]{1,0:T(8,128)(2,1)S(1)} %collective-permute-done.4.refs_2_, ...), custom_call_target="tpu_custom_call" | custom-call | bytes 14680064 | tf_op jit(solution)/shard_map/pallas_call | solution.py:453
  36.0 2.0 %collective-permute-done.11.refs_3_ = bf16[128,1024]{1,0:T(8,128)(2,1)S(1)} collective-permute-done((bf16[128,1024]{1,0:T(8,128)(2,1)S(1)}, bf16[128,1024]{1,0:T(8,128)(2,1)S(1)}, u32[]{:S(2)}, u32[]{:S(2)}) %collective-permute-start.11) | collective-permute-done | bytes 262176 | tf_op jit(solution)/shard_map/ppermute | solution.py:479
  37.9 5.5 %shard_map.88 = (bf16[128,1024]{1,0:T(8,128)(2,1)S(1)}, bf16[128,1024]{1,0:T(8,128)(2,1)S(1)}, bf16[128,1024]{1,0:T(8,128)(2,1)S(1)}, bf16[128,1024]{1,0:T(8,128...) custom-call(s32[1,256]{1,0:T(1,128)S(1)} %get-tuple-element.34.pos_r, ...), custom_call_target="tpu_custom_call" | custom-call | bytes 41943040 | tf_op jit(solution)/shard_map/pallas_call | solution.py:453
  43.4 1.7 %collective-permute-start.12 = (bf16[320,256]{1,0:T(8,128)(2,1)S(1)}, bf16[320,256]{1,0:T(8,128)(2,1)S(1)}, u32[]{:S(2)}, u32[]{:S(2)}) collective-permute-start(bf16[320,256]{1,0:T(8,128)(2,1)S(1)} %get-tuple-element.49), channel_id=1, source_target_pairs={{0,4},{1,5},{2,6},{3,7},{4,0},{5,1},{6,2},{7,3},{8,12},{9,13},{10,... | collective-permute-start | bytes 491528 | tf_op jit(solution)/shard_map/ppermute | solution.py:485
  45.5 3.6 %collective-permute-done.7.refs_7_ = f32[2,8,512]{2,1,0:T(8,128)S(1)} collective-permute-done((f32[2,8,512]{2,1,0:T(8,128)S(1)}, f32[2,8,512]{2,1,0:T(8,128)S(1)}, u32[]{:S(2)}, u32[]{:S(2)}) %collective-permute-start.7) | collective-permute-done | bytes 32800 | tf_op jit(solution)/shard_map/ppermute | solution.py:485
  49.2 4.9 %shard_map.89 = (f32[4,512,256]{2,1,0:T(8,128)S(1)}, bf16[144,1024]{1,0:T(8,128)(2,1)S(1)}, f32[128,1024]{1,0:T(8,128)S(1)}) custom-call(s32[1,256]{1,0:T(1,128)S(1)} %get-tuple-element.34.pos_ref, bf16[512,256]{1,0:T(8,128)(2,1)S(1)} %get-tuple-element.39.refs_0_.kv_ref, bf16[512,256]{1,0:T(8,128)(2,1)S(1)} %collective-permute-done.3.refs_1_, ...), custom_call_target="tpu_custom_call" | custom-call | bytes 25165824 | tf_op jit(solution)/shard_map/pallas_call | solution.py:453
  54.1 1.7 %collective-permute-start.16 = (bf16[144,1024]{1,0:T(8,128)(2,1)S(1)}, bf16[144,1024]{1,0:T(8,128)(2,1)S(1)}, u32[]{:S(2)}, u32[]{:S(2)}) collective-permute-start(bf16[144,1024]{1,0:T(8,128)(2,1)S(1)} %get-tuple-element.55), channel_id=1, source_target_pairs={{0,4},{1,5},{2,6},{3,7},{4,0},{5,1},{6,2},{7,3},{8,12},{9,13},{10,... | collective-permute-start | bytes 884744 | tf_op jit(solution)/shard_map/ppermute | solution.py:485
  56.6 5.1 %collective-permute-start.14 = (bf16[512,256]{1,0:T(8,128)(2,1)S(1)}, bf16[512,256]{1,0:T(8,128)(2,1)S(1)}, u32[]{:S(2)}, u32[]{:S(2)}) collective-permute-start(bf16[512,256]{1,0:T(8,128)(2,1)S(1)} %get-tuple-element.52), channel_id=1, source_target_pairs={{0,16},{1,17},{2,18},{3,19},{4,20},{5,21},{6,22},{7,23},{8,24},{9,... | collective-permute-start | bytes 786440 | tf_op jit(solution)/shard_map/ppermute | solution.py:482
  61.7 1.9 %collective-permute-start.20 = (bf16[128,1024]{1,0:T(8,128)(2,1)S(1)}, bf16[128,1024]{1,0:T(8,128)(2,1)S(1)}, u32[]{:S(2)}, u32[]{:S(2)}) collective-permute-start(bf16[128,1024]{1,0:T(8,128)(2,1)S(1)} %get-tuple-element.61), channel_id=1, source_target_pairs={{0,1},{1,2},{2,3},{3,0},{4,5},{5,6},{6,7},{7,4},{8,9},{9,10},{10,1... | collective-permute-start | bytes 786440 | tf_op jit(solution)/shard_map/ppermute | solution.py:479
  63.6 2.2 %collective-permute-start.21 = (bf16[128,1024]{1,0:T(8,128)(2,1)S(1)}, bf16[128,1024]{1,0:T(8,128)(2,1)S(1)}, u32[]{:S(2)}, u32[]{:S(2)}) collective-permute-start(bf16[128,1024]{1,0:T(8,128)(2,1)S(1)} %get-tuple-element.62), channel_id=1, source_target_pairs={{0,2},{1,3},{2,0},{3,1},{4,6},{5,7},{6,4},{7,5},{8,10},{9,11},{10,... | collective-permute-start | bytes 786440 | tf_op jit(solution)/shard_map/ppermute | solution.py:479
  65.8 5.8 %collective-permute-start.22 = (bf16[128,1024]{1,0:T(8,128)(2,1)S(1)}, bf16[128,1024]{1,0:T(8,128)(2,1)S(1)}, u32[]{:S(2)}, u32[]{:S(2)}) collective-permute-start(bf16[128,1024]{1,0:T(8,128)(2,1)S(1)} %get-tuple-element.63), channel_id=1, source_target_pairs={{0,3},{1,0},{2,1},{3,2},{4,7},{5,4},{6,5},{7,6},{8,11},{9,8},{10,9... | collective-permute-start | bytes 786440 | tf_op jit(solution)/shard_map/ppermute | solution.py:479
  72.3 2.1 %collective-permute-start.18 = (bf16[256,256]{1,0:T(8,128)(2,1)S(1)}, bf16[256,256]{1,0:T(8,128)(2,1)S(1)}, u32[]{:S(2)}, u32[]{:S(2)}) collective-permute-start(bf16[256,256]{1,0:T(8,128)(2,1)S(1)} %get-tuple-element.58), channel_id=1, source_target_pairs={{0,2},{1,3},{2,0},{3,1},{4,6},{5,7},{6,4},{7,5},{8,10},{9,11},{10,... | collective-permute-start | bytes 393224 | tf_op jit(solution)/shard_map/ppermute | solution.py:479
  74.4 1.8 %collective-permute-start.19 = (bf16[256,256]{1,0:T(8,128)(2,1)S(1)}, bf16[256,256]{1,0:T(8,128)(2,1)S(1)}, u32[]{:S(2)}, u32[]{:S(2)}) collective-permute-start(bf16[256,256]{1,0:T(8,128)(2,1)S(1)} %get-tuple-element.59), channel_id=1, source_target_pairs={{0,3},{1,0},{2,1},{3,2},{4,7},{5,4},{6,5},{7,6},{8,11},{9,8},{10,9... | collective-permute-start | bytes 393224 | tf_op jit(solution)/shard_map/ppermute | solution.py:479
  76.2 3.3 %collective-permute-done.22.refs_7_ = bf16[128,1024]{1,0:T(8,128)(2,1)S(1)} collective-permute-done((bf16[128,1024]{1,0:T(8,128)(2,1)S(1)}, bf16[128,1024]{1,0:T(8,128)(2,1)S(1)}, u32[]{:S(2)}, u32[]{:S(2)}) %collective-permute-start.22) | collective-permute-done | bytes 262176 | tf_op jit(solution)/shard_map/ppermute | solution.py:479
  (31 shorter events, 10.7 us)
Async XLA Ops:
  2.3 7.7 %collective-permute-start = (bf16[256,256]{1,0:T(8,128)(2,1)S(1)}, bf16[256,256]{1,0:T(8,128)(2,1)S(1)}, u32[]{:S(2)}, u32[]{:S(2)}) collective-permute-start(bf16[256,256]{1,0:T(8,128)(2,1)S(1)} %get-tuple-element.36), channel_id=1, source_target_pairs={{0,1},{1,2},{2,3},{3,0},{4,5},{5,6},{6,7},{7,4},{8,9},{9,10},{10,1... | collective-permute-start | bytes 393224 | tf_op jit(solution)/shard_map/ppermute | solution.py:479
  4.4 9.6 %collective-permute-start.1 = (bf16[256,256]{1,0:T(8,128)(2,1)S(1)}, bf16[256,256]{1,0:T(8,128)(2,1)S(1)}, u32[]{:S(2)}, u32[]{:S(2)}) collective-permute-start(bf16[256,256]{1,0:T(8,128)(2,1)S(1)} %get-tuple-element.37), channel_id=1, source_target_pairs={{0,2},{1,3},{2,0},{3,1},{4,6},{5,7},{6,4},{7,5},{8,10},{9,11},{10,... | collective-permute-start | bytes 393224 | tf_op jit(solution)/shard_map/ppermute | solution.py:479
  8.0 6.0 %collective-permute-start.2 = (bf16[256,256]{1,0:T(8,128)(2,1)S(1)}, bf16[256,256]{1,0:T(8,128)(2,1)S(1)}, u32[]{:S(2)}, u32[]{:S(2)}) collective-permute-start(bf16[256,256]{1,0:T(8,128)(2,1)S(1)} %get-tuple-element.38), channel_id=1, source_target_pairs={{0,3},{1,0},{2,1},{3,2},{4,7},{5,4},{6,5},{7,6},{8,11},{9,8},{10,9... | collective-permute-start | bytes 393224 | tf_op jit(solution)/shard_map/ppermute | solution.py:479
  14.0 13.2 %collective-permute-start.5 = (bf16[512,256]{1,0:T(8,128)(2,1)S(1)}, bf16[512,256]{1,0:T(8,128)(2,1)S(1)}, u32[]{:S(2)}, u32[]{:S(2)}) collective-permute-start(bf16[512,256]{1,0:T(8,128)(2,1)S(1)} %get-tuple-element.39.refs_0_.kv_ref), channel_id=1, source_target_pairs={{0,24},{1,25},{2,26},{3,27},{4,28},{5,29},{6,30},{7,31},{8,0},{9,1... | collective-permute-start | bytes 786440 | tf_op jit(solution)/shard_map/ppermute | solution.py:482
  16.9 12.4 %collective-permute-start.4 = (bf16[512,256]{1,0:T(8,128)(2,1)S(1)}, bf16[512,256]{1,0:T(8,128)(2,1)S(1)}, u32[]{:S(2)}, u32[]{:S(2)}) collective-permute-start(bf16[512,256]{1,0:T(8,128)(2,1)S(1)} %get-tuple-element.39.refs_0_.kv_ref), channel_id=1, source_target_pairs={{0,16},{1,17},{2,18},{3,19},{4,20},{5,21},{6,22},{7,23},{8,24},{9,... | collective-permute-start | bytes 786440 | tf_op jit(solution)/shard_map/ppermute | solution.py:482
  17.7 14.2 %collective-permute-start.3 = (bf16[512,256]{1,0:T(8,128)(2,1)S(1)}, bf16[512,256]{1,0:T(8,128)(2,1)S(1)}, u32[]{:S(2)}, u32[]{:S(2)}) collective-permute-start(bf16[512,256]{1,0:T(8,128)(2,1)S(1)} %get-tuple-element.39.refs_0_.kv_ref), channel_id=1, source_target_pairs={{0,8},{1,9},{2,10},{3,11},{4,12},{5,13},{6,14},{7,15},{8,16},{9,17... | collective-permute-start | bytes 786440 | tf_op jit(solution)/shard_map/ppermute | solution.py:482
  18.6 15.4 %collective-permute-start.6 = (bf16[576,256]{1,0:T(8,128)(2,1)S(1)}, bf16[576,256]{1,0:T(8,128)(2,1)S(1)}, u32[]{:S(2)}, u32[]{:S(2)}) collective-permute-start(bf16[576,256]{1,0:T(8,128)(2,1)S(1)} %get-tuple-element.40.refs_4_), channel_id=1, source_target_pairs={{0,4},{1,5},{2,6},{3,7},{4,0},{5,1},{6,2},{7,3},{8,12},{9,13},{10,... | collective-permute-start | bytes 884744 | tf_op jit(solution)/shard_map/ppermute | solution.py:485
  20.1 15.8 %collective-permute-start.9 = (bf16[128,1024]{1,0:T(8,128)(2,1)S(1)}, bf16[128,1024]{1,0:T(8,128)(2,1)S(1)}, u32[]{:S(2)}, u32[]{:S(2)}) collective-permute-start(bf16[128,1024]{1,0:T(8,128)(2,1)S(1)} %get-tuple-element.42), channel_id=1, source_target_pairs={{0,1},{1,2},{2,3},{3,0},{4,5},{5,6},{6,7},{7,4},{8,9},{9,10},{10,1... | collective-permute-start | bytes 786440 | tf_op jit(solution)/shard_map/ppermute | solution.py:479
  27.2 8.7 %collective-permute-start.10 = (bf16[128,1024]{1,0:T(8,128)(2,1)S(1)}, bf16[128,1024]{1,0:T(8,128)(2,1)S(1)}, u32[]{:S(2)}, u32[]{:S(2)}) collective-permute-start(bf16[128,1024]{1,0:T(8,128)(2,1)S(1)} %get-tuple-element.43), channel_id=1, source_target_pairs={{0,2},{1,3},{2,0},{3,1},{4,6},{5,7},{6,4},{7,5},{8,10},{9,11},{10,... | collective-permute-start | bytes 786440 | tf_op jit(solution)/shard_map/ppermute | solution.py:479
  29.2 8.7 %collective-permute-start.11 = (bf16[128,1024]{1,0:T(8,128)(2,1)S(1)}, bf16[128,1024]{1,0:T(8,128)(2,1)S(1)}, u32[]{:S(2)}, u32[]{:S(2)}) collective-permute-start(bf16[128,1024]{1,0:T(8,128)(2,1)S(1)} %get-tuple-element.44), channel_id=1, source_target_pairs={{0,3},{1,0},{2,1},{3,2},{4,7},{5,4},{6,5},{7,6},{8,11},{9,8},{10,9... | collective-permute-start | bytes 786440 | tf_op jit(solution)/shard_map/ppermute | solution.py:479
  32.3 5.6 %collective-permute-start.8 = (bf16[320,256]{1,0:T(8,128)(2,1)S(1)}, bf16[320,256]{1,0:T(8,128)(2,1)S(1)}, u32[]{:S(2)}, u32[]{:S(2)}) collective-permute-start(bf16[320,256]{1,0:T(8,128)(2,1)S(1)} %shard_map.87.e2_ref), channel_id=1, source_target_pairs={{0,4},{1,5},{2,6},{3,7},{4,0},{5,1},{6,2},{7,3},{8,12},{9,13},{10,... | collective-permute-start | bytes 491528 | tf_op jit(solution)/shard_map/ppermute | solution.py:485
  43.4 12.4 %collective-permute-start.12 = (bf16[320,256]{1,0:T(8,128)(2,1)S(1)}, bf16[320,256]{1,0:T(8,128)(2,1)S(1)}, u32[]{:S(2)}, u32[]{:S(2)}) collective-permute-start(bf16[320,256]{1,0:T(8,128)(2,1)S(1)} %get-tuple-element.49), channel_id=1, source_target_pairs={{0,4},{1,5},{2,6},{3,7},{4,0},{5,1},{6,2},{7,3},{8,12},{9,13},{10,... | collective-permute-start | bytes 491528 | tf_op jit(solution)/shard_map/ppermute | solution.py:485
  45.1 4.1 %collective-permute-start.7 = (f32[2,8,512]{2,1,0:T(8,128)S(1)}, f32[2,8,512]{2,1,0:T(8,128)S(1)}, u32[]{:S(2)}, u32[]{:S(2)}) collective-permute-start(f32[2,8,512]{2,1,0:T(8,128)S(1)} %shard_map.86.after_ref.refs_6_), channel_id=1, source_target_pairs={{0,4},{1,5},{2,6},{3,7},{4,0},{5,1},{6,2},{7,3},{8,12},{9,13},{10,... | collective-permute-start | bytes 98312 | tf_op jit(solution)/shard_map/ppermute | solution.py:485
  54.1 9.5 %collective-permute-start.16 = (bf16[144,1024]{1,0:T(8,128)(2,1)S(1)}, bf16[144,1024]{1,0:T(8,128)(2,1)S(1)}, u32[]{:S(2)}, u32[]{:S(2)}) collective-permute-start(bf16[144,1024]{1,0:T(8,128)(2,1)S(1)} %get-tuple-element.55), channel_id=1, source_target_pairs={{0,4},{1,5},{2,6},{3,7},{4,0},{5,1},{6,2},{7,3},{8,12},{9,13},{10,... | collective-permute-start | bytes 884744 | tf_op jit(solution)/shard_map/ppermute | solution.py:485
  56.5 9.3 %collective-permute-start.13 = (bf16[512,256]{1,0:T(8,128)(2,1)S(1)}, bf16[512,256]{1,0:T(8,128)(2,1)S(1)}, u32[]{:S(2)}, u32[]{:S(2)}) collective-permute-start(bf16[512,256]{1,0:T(8,128)(2,1)S(1)} %get-tuple-element.51), channel_id=1, source_target_pairs={{0,8},{1,9},{2,10},{3,11},{4,12},{5,13},{6,14},{7,15},{8,16},{9,17... | collective-permute-start | bytes 786440 | tf_op jit(solution)/shard_map/ppermute | solution.py:482
  56.6 15.1 %collective-permute-start.14 = (bf16[512,256]{1,0:T(8,128)(2,1)S(1)}, bf16[512,256]{1,0:T(8,128)(2,1)S(1)}, u32[]{:S(2)}, u32[]{:S(2)}) collective-permute-start(bf16[512,256]{1,0:T(8,128)(2,1)S(1)} %get-tuple-element.52), channel_id=1, source_target_pairs={{0,16},{1,17},{2,18},{3,19},{4,20},{5,21},{6,22},{7,23},{8,24},{9,... | collective-permute-start | bytes 786440 | tf_op jit(solution)/shard_map/ppermute | solution.py:482
  61.7 10.0 %collective-permute-start.15 = (bf16[512,256]{1,0:T(8,128)(2,1)S(1)}, bf16[512,256]{1,0:T(8,128)(2,1)S(1)}, u32[]{:S(2)}, u32[]{:S(2)}) collective-permute-start(bf16[512,256]{1,0:T(8,128)(2,1)S(1)} %get-tuple-element.53), channel_id=1, source_target_pairs={{0,24},{1,25},{2,26},{3,27},{4,28},{5,29},{6,30},{7,31},{8,0},{9,1... | collective-permute-start | bytes 786440 | tf_op jit(solution)/shard_map/ppermute | solution.py:482
  61.7 12.7 %collective-permute-start.20 = (bf16[128,1024]{1,0:T(8,128)(2,1)S(1)}, bf16[128,1024]{1,0:T(8,128)(2,1)S(1)}, u32[]{:S(2)}, u32[]{:S(2)}) collective-permute-start(bf16[128,1024]{1,0:T(8,128)(2,1)S(1)} %get-tuple-element.61), channel_id=1, source_target_pairs={{0,1},{1,2},{2,3},{3,0},{4,5},{5,6},{6,7},{7,4},{8,9},{9,10},{10,1... | collective-permute-start | bytes 786440 | tf_op jit(solution)/shard_map/ppermute | solution.py:479
  63.6 12.6 %collective-permute-start.21 = (bf16[128,1024]{1,0:T(8,128)(2,1)S(1)}, bf16[128,1024]{1,0:T(8,128)(2,1)S(1)}, u32[]{:S(2)}, u32[]{:S(2)}) collective-permute-start(bf16[128,1024]{1,0:T(8,128)(2,1)S(1)} %get-tuple-element.62), channel_id=1, source_target_pairs={{0,2},{1,3},{2,0},{3,1},{4,6},{5,7},{6,4},{7,5},{8,10},{9,11},{10,... | collective-permute-start | bytes 786440 | tf_op jit(solution)/shard_map/ppermute | solution.py:479
  65.8 13.7 %collective-permute-start.22 = (bf16[128,1024]{1,0:T(8,128)(2,1)S(1)}, bf16[128,1024]{1,0:T(8,128)(2,1)S(1)}, u32[]{:S(2)}, u32[]{:S(2)}) collective-permute-start(bf16[128,1024]{1,0:T(8,128)(2,1)S(1)} %get-tuple-element.63), channel_id=1, source_target_pairs={{0,3},{1,0},{2,1},{3,2},{4,7},{5,4},{6,5},{7,6},{8,11},{9,8},{10,9... | collective-permute-start | bytes 786440 | tf_op jit(solution)/shard_map/ppermute | solution.py:479
  72.2 7.7 %collective-permute-start.17 = (bf16[256,256]{1,0:T(8,128)(2,1)S(1)}, bf16[256,256]{1,0:T(8,128)(2,1)S(1)}, u32[]{:S(2)}, u32[]{:S(2)}) collective-permute-start(bf16[256,256]{1,0:T(8,128)(2,1)S(1)} %get-tuple-element.57), channel_id=1, source_target_pairs={{0,1},{1,2},{2,3},{3,0},{4,5},{5,6},{6,7},{7,4},{8,9},{9,10},{10,1... | collective-permute-start | bytes 393224 | tf_op jit(solution)/shard_map/ppermute | solution.py:479
  72.3 7.6 %collective-permute-start.18 = (bf16[256,256]{1,0:T(8,128)(2,1)S(1)}, bf16[256,256]{1,0:T(8,128)(2,1)S(1)}, u32[]{:S(2)}, u32[]{:S(2)}) collective-permute-start(bf16[256,256]{1,0:T(8,128)(2,1)S(1)} %get-tuple-element.58), channel_id=1, source_target_pairs={{0,2},{1,3},{2,0},{3,1},{4,6},{5,7},{6,4},{7,5},{8,10},{9,11},{10,... | collective-permute-start | bytes 393224 | tf_op jit(solution)/shard_map/ppermute | solution.py:479
  74.4 7.0 %collective-permute-start.19 = (bf16[256,256]{1,0:T(8,128)(2,1)S(1)}, bf16[256,256]{1,0:T(8,128)(2,1)S(1)}, u32[]{:S(2)}, u32[]{:S(2)}) collective-permute-start(bf16[256,256]{1,0:T(8,128)(2,1)S(1)} %get-tuple-element.59), channel_id=1, source_target_pairs={{0,3},{1,0},{2,1},{3,2},{4,7},{5,4},{6,5},{7,6},{8,11},{9,8},{10,9... | collective-permute-start | bytes 393224 | tf_op jit(solution)/shard_map/ppermute | solution.py:479
